TPU v7x, 32 devices: a whole 2x2x4 slice. The times are simulated.
32 devices in a mesh: dp: 8 (over z, y), seq: 4 (over x, core).
Axes of the slice: x: 2, y: 2, z: 4, core: 2. Of those that a mesh axis runs over, the one named last changes fastest.
Arguments:
- residual: float32 [8192, 768], P(('dp', 'seq')), may hold values from -6 to 6
- cotangent: float32 [8192, 768], P(('dp', 'seq')), may hold values from -6 to 6
- segments: int32 [8192], P('dp'), may hold values from 0 to 15, as said below
- triple_weight: float32 [2, 768, 2304], P(None, 'dp', 'seq'), may hold values from -0.21875 to 0.21875
- triple_moment: float32 [2, 768, 2304], P(None, 'dp', 'seq'), may hold values from -0.33 to 0.33
- triple_square: float32 [2, 768, 2304], P(None, 'dp', 'seq'), may hold values from 0.00025 to 0.001
- triple_shadow: float32 [2, 768, 2304], P(None, 'dp', 'seq'), may hold values from -0.21875 to 0.21875
- output_weight: float32 [2, 768, 768], P(None, 'dp', 'seq'), may hold values from -0.875 to 0.875
- output_moment: float32 [2, 768, 768], P(None, 'dp', 'seq'), may hold values from -0.33 to 0.33
- output_square: float32 [2, 768, 768], P(None, 'dp', 'seq'), may hold values from 0.00025 to 0.001
- output_shadow: float32 [2, 768, 768], P(None, 'dp', 'seq'), may hold values from -0.875 to 0.875
- expand_weight: float32 [2, 768, 3072], P(None, 'dp', 'seq'), may hold values from -0.21875 to 0.21875
- expand_moment: float32 [2, 768, 3072], P(None, 'dp', 'seq'), may hold values from -0.33 to 0.33
- expand_square: float32 [2, 768, 3072], P(None, 'dp', 'seq'), may hold values from 0.00025 to 0.001
- expand_shadow: float32 [2, 768, 3072], P(None, 'dp', 'seq'), may hold values from -0.21875 to 0.21875
- shrink_weight: float32 [2, 3072, 768], P(None, 'dp', 'seq'), may hold values from -0.109375 to 0.109375
- shrink_moment: float32 [2, 3072, 768], P(None, 'dp', 'seq'), may hold values from -0.33 to 0.33
- shrink_square: float32 [2, 3072, 768], P(None, 'dp', 'seq'), may hold values from 0.00025 to 0.001
- shrink_shadow: float32 [2, 3072, 768], P(None, 'dp', 'seq'), may hold values from -0.109375 to 0.109375
- scales_weight: float32 [2, 4, 768], P(None, 'seq', 'dp'), may hold values from -0.5 to 2.3
- scales_moment: float32 [2, 4, 768], P(None, 'seq', 'dp'), may hold values from -0.33 to 0.33
- scales_square: float32 [2, 4, 768], P(None, 'seq', 'dp'), may hold values from 0.00025 to 0.32
- scales_shadow: float32 [2, 4, 768], P(None, 'seq', 'dp'), may hold values from -0.5 to 2.3
Outputs:
- block_out: float32 [8192, 768], P(('dp', 'seq'))
- input_grad: float32 [8192, 768], P(('dp', 'seq'))
- grad_norm: float32 [], replicated
- triple_updated: float32 [2, 768, 2304], P(None, 'dp', 'seq')
- triple_momentum: float32 [2, 768, 2304], P(None, 'dp', 'seq')
- triple_variance: float32 [2, 768, 2304], P(None, 'dp', 'seq')
- triple_average: float32 [2, 768, 2304], P(None, 'dp', 'seq')
- output_updated: float32 [2, 768, 768], P(None, 'dp', 'seq')
- output_momentum: float32 [2, 768, 768], P(None, 'dp', 'seq')
- output_variance: float32 [2, 768, 768], P(None, 'dp', 'seq')
- output_average: float32 [2, 768, 768], P(None, 'dp', 'seq')
- expand_updated: float32 [2, 768, 3072], P(None, 'dp', 'seq')
- expand_momentum: float32 [2, 768, 3072], P(None, 'dp', 'seq')
- expand_variance: float32 [2, 768, 3072], P(None, 'dp', 'seq')
- expand_average: float32 [2, 768, 3072], P(None, 'dp', 'seq')
- shrink_updated: float32 [2, 3072, 768], P(None, 'dp', 'seq')
- shrink_momentum: float32 [2, 3072, 768], P(None, 'dp', 'seq')
- shrink_variance: float32 [2, 3072, 768], P(None, 'dp', 'seq')
- shrink_average: float32 [2, 3072, 768], P(None, 'dp', 'seq')
- scales_updated: float32 [2, 4, 768], P(None, 'seq', 'dp')
- scales_momentum: float32 [2, 4, 768], P(None, 'seq', 'dp')
- scales_variance: float32 [2, 4, 768], P(None, 'seq', 'dp')
- scales_average: float32 [2, 4, 768], P(None, 'seq', 'dp')
Inputs may be any that keep to these rules, and one draw needn't show every extreme that they name: Ids never fall along the tokens; each aligned block of 1024 tokens holds whole segments only, and ids of different blocks differ; every segment has 1024 or half of 1024 tokens and starts at a multiple of half of 1024 within its block; ids need not be consecutive.
All inputs are finite; a program needn't handle non-finite values.
Results may differ from a plain program's by a relative error of at most 0.02.
Values may be sent and summed in bfloat16 or wider, within the bound.
A program may use at most 192 MiB of HBM per device.

v0:
```python
import functools
import math
from typing import Any, NamedTuple

import jax
import jax.numpy as jnp
from jax import lax
from jax.experimental import pallas as pl
from jax.experimental.pallas import tpu as pltpu
from jax.sharding import PartitionSpec as P

D = 768
FF = 3072
HD = 64
LAYERS = 2
STEP = 2
SEQ = 4

EPSILON = 1e-05
ROTARY_BASE = 10000.0
BETA_ONE = 0.9
BETA_TWO = 0.999
ADAM_EPSILON = 1e-08
DECAY_RATE = 0.01
SHADOW_RATE = 0.99
CLIP_RATIO = 0.5
RATE_FACTOR = 1.5
SCALES_RATE = 0.6
MASKED = -1000000000.0

HALF = D // 2
TRI = 3 * HALF
HID = FF // 2
BF = jnp.bfloat16
F32 = jnp.float32
MESH = pl.DeviceIdType.MESH
VMEM_BYTES = 60 << 20


def adam_step(weight, moment, square, shadow, gradient, step_rate):
    shadow_decay = min(SHADOW_RATE, (1.0 + STEP) / (10.0 + STEP))
    momentum = BETA_ONE * moment + (1.0 - BETA_ONE) * gradient
    variance = BETA_TWO * square + (1.0 - BETA_TWO) * gradient * gradient
    corrected = (
        momentum
        / (1.0 - BETA_ONE**STEP)
        / (jnp.sqrt(variance / (1.0 - BETA_TWO**STEP)) + ADAM_EPSILON)
    )
    updated = weight - step_rate * (corrected + DECAY_RATE * weight)
    average = shadow_decay * shadow + (1.0 - shadow_decay) * updated
    return (updated, momentum, variance, average)


def nn(a, b):
    return lax.dot_general(a, b, (((1,), (0,)), ((), ())), preferred_element_type=F32)


def nt(a, b):
    return lax.dot_general(a, b, (((1,), (1,)), ((), ())), preferred_element_type=F32)


def tn(a, b):
    return lax.dot_general(a, b, (((0,), (0,)), ((), ())), preferred_element_type=F32)


def place():
    s = lax.axis_index("seq")
    x = lax.div(s, 2)
    c = lax.rem(s, 2)
    return lax.axis_index("dp"), x, c, lax.rem(s + 2, SEQ), s + 1 - 2 * c


def greet(d, peer, sib):
    barrier = pltpu.get_barrier_semaphore()
    for other in (peer, sib):
        pl.semaphore_signal(barrier, inc=1, device_id=(d, other), device_id_type=MESH)
    pl.semaphore_wait(barrier, 2)


def rows_of(c, n):
    return pl.ds(pl.multiple_of(c * n, n), n)


class Copies:
    def __init__(self, lsem, ssem, rsem, d):
        self.lsem, self.ssem, self.rsem, self.d = lsem, ssem, rsem, d
        self.n_local = 0
        self.n_remote = 0

    def local(self, src, dst):
        copy = pltpu.make_async_copy(src, dst, self.lsem.at[self.n_local])
        self.n_local += 1
        copy.start()
        return copy

    def push(self, src, dst, to):
        copy = pltpu.make_async_remote_copy(
            src_ref=src,
            dst_ref=dst,
            send_sem=self.ssem.at[self.n_remote],
            recv_sem=self.rsem.at[self.n_remote],
            device_id=(self.d, to),
            device_id_type=MESH,
        )
        self.n_remote += 1
        copy.start()
        return copy


def norm_stats(values):
    center = values - jnp.mean(values, axis=-1, keepdims=True)
    spread = jnp.mean(center * center, axis=-1, keepdims=True)
    scale = lax.rsqrt(spread + EPSILON)
    return center * scale, scale


def norm_back(values, gain, dy):
    xhat, scale = norm_stats(values)
    u = gain * dy
    du = u - jnp.mean(u, axis=-1, keepdims=True)
    back = scale * (du - xhat * jnp.mean(u * xhat, axis=-1, keepdims=True))
    rows = jnp.concatenate(
        [jnp.sum(xhat * dy, axis=0, keepdims=True), jnp.sum(dy, axis=0, keepdims=True)], axis=0
    )
    return back, rows


def turn(chunk, cosine, sine):
    lane = lax.broadcasted_iota(jnp.int32, chunk.shape, 1)
    swapped = jnp.where(
        lax.rem(lane, HD) < HD // 2, pltpu.roll(chunk, 128 - HD // 2, 1), pltpu.roll(chunk, HD // 2, 1)
    )
    return chunk * cosine + swapped * sine


def half_of(pair, which):
    lane = lax.broadcasted_iota(jnp.int32, pair.shape, 1)
    keep = (lane < HD) if which == 0 else (lane >= HD)
    return jnp.where(keep, pair, jnp.zeros_like(pair))


def attend_fwd_kernel(
    h, wa, sc, cs, bias, mid, na_o, q_o, k_o, v_o, ctx_o, lse_o,
    wt, wo, na, q, k, v, ctxt, ctx, lse, psend, precv, lsem, ssem, rsem,
):
    d, x, c, peer, sib = place()
    y = 1 - x
    rows = h.shape[0]
    copies = Copies(lsem, ssem, rsem, d)
    greet(d, peer, sib)
    wt_own, wo_own = wt.at[rows_of(c, HALF), :], wo.at[:, rows_of(c, HALF)]
    tri_part, out_part = wa.at[:, pl.ds(0, TRI)], wa.at[:, pl.ds(TRI, HALF)]
    tri_sent = copies.push(tri_part, wt_own, sib)
    tri_local = copies.local(tri_part, wt_own)
    out_sent = copies.push(out_part, wo_own, sib)
    out_local = copies.local(out_part, wo_own)
    xhat, _ = norm_stats(h[...])
    na[x] = (xhat * sc[0:1, :] + sc[1:2, :]).astype(BF)
    na_sent = copies.push(na.at[x], na.at[x], peer)
    tri_local.wait()
    tri_sent.wait()

    def project(block):
        cosine, sine = cs[block, :, 0:128], cs[block, :, 128:256]
        for j in range(9):
            part = nn(na[block], wt[:, 128 * j : 128 * j + 128])
            lanes = pl.ds(128 * (j % 3), 128)
            if j < 3:
                q[block, :, lanes] = (turn(part, cosine, sine) * HD**-0.5).astype(BF)
            elif j < 6:
                k[block, rows_of(c, rows), lanes] = turn(part, cosine, sine).astype(BF)
            else:
                v[block, rows_of(c, rows), lanes] = part.astype(BF)

    def share(block):
        mine = (block, rows_of(c, rows))
        return [copies.push(k.at[mine], k.at[mine], sib), copies.push(v.at[mine], v.at[mine], sib)]

    project(x)
    shared = share(x)
    na_sent.wait()
    project(y)
    shared += share(y)
    out_local.wait()
    out_sent.wait()
    for copy in shared:
        copy.wait()

    def attend(block):
        other = 1 - block

        def pair_step(p, carry):
            lanes = pl.ds(pl.multiple_of(p * 128, 128), 128)
            q_pair = q[block, :, lanes]
            k_same, k_cross = k[block, :, lanes], k[other, :, lanes]
            v_same, v_cross = v[block, :, lanes], v[other, :, lanes]
            for which in range(2):
                q_head = half_of(q_pair, which)
                s_same = nt(k_same, q_head)
                s_cross = nt(k_cross, q_head) + bias[0]
                top = jnp.maximum(
                    jnp.max(s_same, axis=0, keepdims=True), jnp.max(s_cross, axis=0, keepdims=True)
                )
                e_same = jnp.exp(s_same - top)
                e_cross = jnp.exp(s_cross - top)
                total = jnp.sum(e_same, axis=0, keepdims=True) + jnp.sum(
                    e_cross, axis=0, keepdims=True
                )
                mixed = tn(v_same, e_same.astype(BF)) + tn(v_cross, e_cross.astype(BF))
                head = pl.ds(pl.multiple_of(p * 128 + which * HD, HD), HD)
                ctxt[head, :] = mixed[which * HD : which * HD + HD, :] / total
                lse[block, pl.ds(2 * p + which, 1), :] = top + jnp.log(total)
            return carry

        lax.fori_loop(0, HALF // 128, pair_step, 0)
        ctx[block] = ctxt[...].T.astype(BF)
        return nn(ctx[block], wo[...])

    psend[...] = attend(y).astype(BF)
    part_sent = copies.push(psend, precv, peer)
    mid[...] = h[...] + attend(x)
    saves = [
        copies.local(a, b)
        for a, b in ((na, na_o), (q, q_o), (k, k_o), (v, v_o), (ctx, ctx_o), (lse, lse_o))
    ]
    part_sent.wait()
    mid[...] = mid[...] + precv[...].astype(F32)
    for copy in saves:
        copy.wait()


def hbm():
    return pl.BlockSpec(memory_space=pl.ANY)


def vmem():
    return pl.BlockSpec(memory_space=pltpu.VMEM)


def call(kernel, name, number, ins, outs, out_shape, scratch, n_local, n_remote, flops, args):
    return pl.pallas_call(
        kernel,
        name=name,
        out_shape=out_shape,
        in_specs=ins,
        out_specs=outs,
        scratch_shapes=[
            *scratch,
            pltpu.SemaphoreType.DMA((n_local,)),
            pltpu.SemaphoreType.DMA((n_remote,)),
            pltpu.SemaphoreType.DMA((n_remote,)),
        ],
        cost_estimate=pl.CostEstimate(flops=flops, bytes_accessed=16 << 20, transcendentals=0),
        compiler_params=pltpu.CompilerParams(
            collective_id=number, has_side_effects=True, vmem_limit_bytes=VMEM_BYTES
        ),
    )(*args)


def sds(shape, dtype):
    return jax.ShapeDtypeStruct(shape, dtype)


def attend_fwd(h, wa, scales, tables, bias):
    t = h.shape[0]
    return call(
        attend_fwd_kernel, "attend_fwd", 0,
        [vmem(), hbm(), vmem(), vmem(), pl.BlockSpec(memory_space=pltpu.SMEM)],
        [vmem()] + [hbm()] * 6,
        [
            sds((t, D), F32), sds((2, t, D), BF), sds((2, t, HALF), BF), sds((2, 2 * t, HALF), BF),
            sds((2, 2 * t, HALF), BF), sds((2, t, HALF), BF), sds((2, 8, t), F32),
        ],
        [
            pltpu.VMEM((D, TRI), BF), pltpu.VMEM((HALF, D), BF), pltpu.VMEM((2, t, D), BF),
            pltpu.VMEM((2, t, HALF), BF), pltpu.VMEM((2, 2 * t, HALF), BF),
            pltpu.VMEM((2, 2 * t, HALF), BF), pltpu.VMEM((HALF, t), F32),
            pltpu.VMEM((2, t, HALF), BF), pltpu.VMEM((2, 8, t), F32),
            pltpu.VMEM((t, D), BF), pltpu.VMEM((t, D), BF),
        ],
        8, 8, 6 << 30, (h, wa, scales, tables, bias),
    )


def gelu_parts(hidden):
    phi_cap = 0.5 * (1.0 + lax.erf(hidden * math.sqrt(0.5)))
    density = jnp.exp(-0.5 * hidden * hidden) * (1.0 / math.sqrt(2.0 * math.pi))
    return hidden * phi_cap, phi_cap + hidden * density


def feed_fwd_kernel(
    mid, wf, sc, h_next, nb_o, act_o, slope_o,
    we, ws, nb, act, slope, psend, precv, lsem, ssem, rsem,
):
    d, x, c, peer, sib = place()
    y = 1 - x
    copies = Copies(lsem, ssem, rsem, d)
    greet(d, peer, sib)
    xhat, _ = norm_stats(mid[...])
    nb[x] = (xhat * sc[2:3, :] + sc[3:4, :]).astype(BF)
    nb_sent = copies.push(nb.at[x], nb.at[x], peer)
    we_own, ws_own = we.at[:, rows_of(c, D)], ws.at[rows_of(c, D), :]
    exp_part, shr_part = wf.at[:, pl.ds(0, D)], wf.at[:, pl.ds(D, D)]
    weights = [
        copies.local(exp_part, we_own),
        copies.push(exp_part, we_own, sib),
        copies.local(shr_part, ws_own),
        copies.push(shr_part, ws_own, sib),
    ]
    for copy in weights:
        copy.wait()

    def feed(block):
        def step(i, carry):
            lanes = pl.ds(pl.multiple_of(i * 256, 256), 256)
            value, rate = gelu_parts(nn(nb[block], we[:, lanes]))
            act[block, :, lanes] = value.astype(BF)
            slope[block, :, lanes] = rate.astype(BF)
            return carry

        lax.fori_loop(0, HID // 256, step, 0)
        return nn(act[block], ws[...])

    h_next[...] = mid[...] + feed(x)
    nb_sent.wait()
    psend[...] = feed(y).astype(BF)
    part_sent = copies.push(psend, precv, peer)
    saves = [copies.local(a, b) for a, b in ((nb, nb_o), (act, act_o), (slope, slope_o))]
    part_sent.wait()
    h_next[...] = h_next[...] + precv[...].astype(F32)
    for copy in saves:
        copy.wait()


def feed_fwd(mid, wf, scales):
    t = mid.shape[0]
    return call(
        feed_fwd_kernel, "feed_fwd", 1,
        [vmem(), hbm(), vmem()],
        [vmem()] + [hbm()] * 3,
        [sds((t, D), F32), sds((2, t, D), BF), sds((2, t, HID), BF), sds((2, t, HID), BF)],
        [
            pltpu.VMEM((D, HID), BF), pltpu.VMEM((HID, D), BF), pltpu.VMEM((2, t, D), BF),
            pltpu.VMEM((2, t, HID), BF), pltpu.VMEM((2, t, HID), BF),
            pltpu.VMEM((t, D), BF), pltpu.VMEM((t, D), BF),
        ],
        5, 4, 5 << 30, (mid, wf, scales),
    )


def feed_bwd_kernel(
    g, mid, wf, sc, nb_h, act_h, slope_h, mid_grad, wg_o, rows_o,
    we, ws, nb, act, slope, gl, hg, part, psend, precv, gown, gsend, grecv, lsem, ssem, rsem,
):
    d, x, c, peer, sib = place()
    y = 1 - x
    t = g.shape[0]
    copies = Copies(lsem, ssem, rsem, d)
    greet(d, peer, sib)
    gl[x] = g[...].astype(BF)
    g_sent = copies.push(gl.at[x], gl.at[x], peer)
    we_own, ws_own = we.at[:, rows_of(c, D)], ws.at[rows_of(c, D), :]
    exp_part, shr_part = wf.at[:, pl.ds(0, D)], wf.at[:, pl.ds(D, D)]
    weights = [
        copies.local(shr_part, ws_own),
        copies.push(shr_part, ws_own, sib),
        copies.local(exp_part, we_own),
        copies.push(exp_part, we_own, sib),
        copies.local(slope_h, slope),
        copies.local(act_h, act),
        copies.local(nb_h, nb),
    ]
    for copy in weights:
        copy.wait()

    def back(block):
        def step(i, carry):
            lanes = pl.ds(pl.multiple_of(i * 256, 256), 256)
            pulled = nt(gl[block], ws[lanes, :])
            hg[block, :, lanes] = (pulled * slope[block, :, lanes].astype(F32)).astype(BF)
            return carry

        lax.fori_loop(0, HID // 256, step, 0)
        return nt(hg[block], we[...])

    part[...] = back(x)
    g_sent.wait()
    psend[...] = back(y).astype(BF)
    part_sent = copies.push(psend, precv, peer)

    gl_all = gl[...].reshape(2 * t, D)
    nb_all = nb[...].reshape(2 * t, D)

    def grads(which, store):
        def step(i, carry):
            at = pl.ds(pl.multiple_of(i * 256, 256), 256)
            off = pl.ds(pl.multiple_of(which * D + i * 256, 256), 256)
            hg_part = hg[:, :, off].reshape(2 * t, 256)
            act_part = act[:, :, off].reshape(2 * t, 256)
            store(0, at, tn(nb_all, hg_part))
            store(1, at, tn(act_part, gl_all))
            return carry

        lax.fori_loop(0, D // 256, step, 0)

    def to_send(kind, at, value):
        if kind == 0:
            gsend[:, at] = value.astype(BF)
        else:
            gsend[at, pl.ds(D, D)] = value.astype(BF)

    def to_keep(kind, at, value):
        if kind == 0:
            gown[:, at] = value
        else:
            gown[at, pl.ds(D, D)] = value

    grads(1 - c, to_send)
    grad_sent = copies.push(gsend, grecv, sib)
    grads(c, to_keep)
    part_sent.wait()
    dy = part[...] + precv[...].astype(F32)
    back_mid, rows = norm_back(mid[...], sc[2:3, :], dy)
    mid_grad[...] = g[...] + back_mid
    rows_o[...] = rows
    grad_sent.wait()
    gsend[...] = (gown[...] + grecv[...].astype(F32)).astype(BF)
    copies.local(gsend, wg_o).wait()


def feed_bwd(g, mid, wf, scales, nb, act, slope):
    t = g.shape[0]
    return call(
        feed_bwd_kernel, "feed_bwd", 2,
        [vmem(), vmem(), hbm(), vmem(), hbm(), hbm(), hbm()],
        [vmem(), hbm(), vmem()],
        [sds((t, D), F32), sds((D, 2 * D), BF), sds((2, D), F32)],
        [
            pltpu.VMEM((D, HID), BF), pltpu.VMEM((HID, D), BF), pltpu.VMEM((2, t, D), BF),
            pltpu.VMEM((2, t, HID), BF), pltpu.VMEM((2, t, HID), BF), pltpu.VMEM((2, t, D), BF),
            pltpu.VMEM((2, t, HID), BF), pltpu.VMEM((t, D), F32), pltpu.VMEM((t, D), BF),
            pltpu.VMEM((t, D), BF), pltpu.VMEM((D, 2 * D), F32), pltpu.VMEM((D, 2 * D), BF),
            pltpu.VMEM((D, 2 * D), BF),
        ],
        6, 5, 10 << 30, (g, mid, wf, scales, nb, act, slope),
    )


def attend_bwd_kernel(
    mg, h, wa, sc, cs, bias, na, q, k, v, ctx, lse, g_prev, wg_o, rows_o,
    wt, wo, ml, cg, delta, dqt, dk, dv, kvsend, kvrecv, pg, part, psend, precv,
    gown, gsend, grecv, lsem, ssem, rsem,
):
    d, x, c, peer, sib = place()
    y = 1 - x
    t = mg.shape[0]
    copies = Copies(lsem, ssem, rsem, d)
    greet(d, peer, sib)
    ml[x] = mg[...].astype(BF)
    ml_sent = copies.push(ml.at[x], ml.at[x], peer)
    wt_own, wo_own = wt.at[rows_of(c, HALF), :], wo.at[:, rows_of(c, HALF)]
    tri_part, out_part = wa.at[:, pl.ds(0, TRI)], wa.at[:, pl.ds(TRI, HALF)]
    out_moves = [copies.local(out_part, wo_own), copies.push(out_part, wo_own, sib)]
    tri_moves = [copies.local(tri_part, wt_own), copies.push(tri_part, wt_own, sib)]
    dk[...] = jnp.zeros_like(dk)
    dv[...] = jnp.zeros_like(dv)
    for copy in out_moves:
        copy.wait()

    def attend(block):
        other = 1 - block
        pulled = nt(ml[block], wo[...])
        cg[block] = pulled.astype(BF)
        weighed = (cg[block].astype(F32) * ctx[block].astype(F32)).T
        for head in range(HALF // HD):
            delta[head : head + 1, :] = jnp.sum(
                weighed[head * HD : head * HD + HD, :], axis=0, keepdims=True
            )

        def pair_step(p, carry):
            lanes = pl.ds(pl.multiple_of(p * 128, 128), 128)
            q_pair, cg_pair = q[block, :, lanes], cg[block, :, lanes]
            for which in range(2):
                q_head, cg_head = half_of(q_pair, which), half_of(cg_pair, which)
                row = pl.ds(2 * p + which, 1)
                total, dots = lse[block, row, :], delta[row, :]
                turned = None
                for side in (block, other):
                    k_pair, v_pair = k[side, :, lanes], v[side, :, lanes]
                    scores = nt(k_pair, q_head)
                    if side is other:
                        scores = scores + bias[0]
                    probs = jnp.exp(scores - total)
                    score_grad = (probs * (nt(v_pair, cg_head) - dots)).astype(BF)
                    dv[side, :, lanes] += nn(probs.astype(BF), cg_head)
                    dk[side, :, lanes] += nn(score_grad, q_head)
                    piece = tn(k_pair, score_grad)
                    turned = piece if turned is None else turned + piece
                head = pl.ds(pl.multiple_of(p * 128 + which * HD, HD), HD)
                dqt[block, head, :] = turned[which * HD : which * HD + HD, :] * HD**-0.5
            return carry

        lax.fori_loop(0, HALF // 128, pair_step, 0)

    attend(x)
    ml_sent.wait()
    attend(y)
    theirs, mine = rows_of(1 - c, t), rows_of(c, t)
    for side in range(2):
        kvsend[side, :, pl.ds(0, HALF)] = dk[side, theirs, :].astype(BF)
        kvsend[side, :, pl.ds(HALF, HALF)] = dv[side, theirs, :].astype(BF)
    kv_sent = copies.push(kvsend, kvrecv, sib)

    def unturn(block, j, value):
        cosine, sine = cs[block, :, 0:128], cs[block, :, 128:256]
        rounded = value.astype(BF).astype(F32)
        pg[block, :, pl.ds(128 * j, 128)] = turn(rounded, cosine, -sine).astype(BF)

    for side in range(2):
        for j in range(3):
            unturn(side, j, dqt[side, 128 * j : 128 * j + 128, :].T)
    kv_sent.wait()
    for side in range(2):
        for j in range(3):
            at = pl.ds(128 * j, 128)
            unturn(side, 3 + j, dk[side, mine, at] + kvrecv[side, :, at].astype(F32))
            pg[side, :, pl.ds(D + 128 * j, 128)] = (
                dv[side, mine, at] + kvrecv[side, :, pl.ds(HALF + 128 * j, 128)].astype(F32)
            ).astype(BF)
    for copy in tri_moves:
        copy.wait()
    psend[...] = nt(pg[y], wt[...]).astype(BF)
    part_sent = copies.push(psend, precv, peer)
    part[...] = nt(pg[x], wt[...])

    ml_all = ml[...].reshape(2 * t, D)
    na_all = na[...].reshape(2 * t, D)
    ctx_all = ctx[...].reshape(2 * t, HALF)

    def grads(which, store):
        def step(i, carry):
            off = pl.ds(pl.multiple_of(which * HALF + i * 128, 128), 128)
            at = pl.ds(pl.multiple_of(i * 128, 128), 128)
            store(0, at, tn(na[:, :, off].reshape(2 * t, 128), pg[...].reshape(2 * t, TRI)))
            store(1, at, tn(ctx_all, ml[:, :, off].reshape(2 * t, 128)))
            return carry

        lax.fori_loop(0, HALF // 128, step, 0)

    def to_send(kind, at, value):
        if kind == 0:
            gsend[at, pl.ds(0, TRI)] = value.astype(BF)
        else:
            gsend[:, pl.ds(pl.multiple_of(TRI + at.start, 128), 128)] = value.astype(BF)

    def to_keep(kind, at, value):
        if kind == 0:
            gown[at, pl.ds(0, TRI)] = value
        else:
            gown[:, pl.ds(pl.multiple_of(TRI + at.start, 128), 128)] = value

    grads(1 - c, to_send)
    grad_sent = copies.push(gsend, grecv, sib)
    grads(c, to_keep)
    part_sent.wait()
    dy = part[...] + precv[...].astype(F32)
    back, rows = norm_back(h[...], sc[0:1, :], dy)
    g_prev[...] = mg[...] + back
    rows_o[...] = rows
    grad_sent.wait()
    gsend[...] = (gown[...] + grecv[...].astype(F32)).astype(BF)
    copies.local(gsend, wg_o).wait()


def attend_bwd(mg, h, wa, scales, tables, bias, saved):
    t = mg.shape[0]
    return call(
        attend_bwd_kernel, "attend_bwd", 3,
        [vmem(), vmem(), hbm(), vmem(), vmem(), pl.BlockSpec(memory_space=pltpu.SMEM)] + [vmem()] * 6,
        [vmem(), hbm(), vmem()],
        [sds((t, D), F32), sds((HALF, 2 * D), BF), sds((2, D), F32)],
        [
            pltpu.VMEM((D, TRI), BF), pltpu.VMEM((HALF, D), BF), pltpu.VMEM((2, t, D), BF),
            pltpu.VMEM((2, t, HALF), BF), pltpu.VMEM((8, t), F32), pltpu.VMEM((2, HALF, t), F32),
            pltpu.VMEM((2, 2 * t, HALF), F32), pltpu.VMEM((2, 2 * t, HALF), F32),
            pltpu.VMEM((2, t, D), BF), pltpu.VMEM((2, t, D), BF), pltpu.VMEM((2, t, TRI), BF),
            pltpu.VMEM((t, D), F32), pltpu.VMEM((t, D), BF), pltpu.VMEM((t, D), BF),
            pltpu.VMEM((HALF, 2 * D), F32), pltpu.VMEM((HALF, 2 * D), BF),
            pltpu.VMEM((HALF, 2 * D), BF),
        ],
        3, 6, 10 << 30, (mg, h, wa, scales, tables, bias, *saved),
    )


TRIPLE, OUTPUT, EXPAND, SHRINK = range(4)
KINDS = (TRIPLE, OUTPUT, EXPAND, SHRINK)
ZS = 4


class Spot:
    def __init__(self):
        s = lax.axis_index("seq")
        self.s = s
        self.x, self.c = lax.div(s, 2), lax.rem(s, 2)
        self.d = lax.axis_index("dp")
        self.z, self.y = lax.div(self.d, 2), lax.rem(self.d, 2)
        self.upper, self.odd = lax.div(self.z, 2), lax.rem(self.z, 2)
        self.sib, self.peer = s + 1 - 2 * self.c, lax.rem(s + 2, SEQ)
        self.across = self.d + 1 - 2 * self.y
        self.zs = ZS

    def count(self, kind):
        return ZS if kind == EXPAND else ZS // 2

    def origin(self, kind, j):
        if kind == TRIPLE:
            return 2 * self.c + j
        if kind == OUTPUT:
            return 2 * self.x + j
        return j if kind == EXPAND else 2 * j + self.x

    def own_slot(self, kind):
        return {TRIPLE: self.odd, OUTPUT: self.odd, EXPAND: self.z, SHRINK: self.upper}[kind]

    def if_owner(self, kind, act):
        if kind == EXPAND:
            act()
        elif kind == TRIPLE:
            pl.when(self.c == self.upper)(act)
        elif kind == OUTPUT:
            pl.when(self.x == self.upper)(act)
        else:
            pl.when(self.x == self.odd)(act)

    def naturals(self, kind):
        x, c = self.x, self.c
        if kind == TRIPLE:
            return ((0, 2 * x), (1, 2 * x + 1), (2, 2 * (1 - x)), (3, 2 * (1 - x) + 1))
        if kind == EXPAND:
            return ((0, 2 * c + x),)
        return ((0, 2 * c), (1, 2 * c + 1))

    def targets(self, kind):
        x, c = self.x, self.c
        if kind == TRIPLE:
            return ((c, 0, 2 * x + self.upper), (2 + c, 1, 2 * (1 - x) + self.upper))
        if kind == OUTPUT:
            return ((c, 0, 2 * self.upper + x),)
        if kind == EXPAND:
            return ((0, 0, 2 * c + x),)
        return ((c, 0, 2 * self.odd + x),)


class Saved(NamedTuple):
    na: Any
    q: Any
    k: Any
    v: Any
    ctx: Any
    ctx_t: Any
    lse: Any
    nb: Any
    act: Any
    slope: Any
    wt: Any
    wo: Any
    we: Any
    ws: Any


class ForwardIn(NamedTuple):
    h0: Any
    sc_own: Any
    cs: Any
    bias: Any
    p_whole: Any
    p_half: Any
    p_out: Any
    p_exp: Any
    p_shr: Any


class ForwardHead(NamedTuple):
    h_out: Any
    h_mid: Any
    mid_o0: Any
    mid_o1: Any
    sc_o: Any


class ForwardScratch(NamedTuple):
    wt: Any
    wo: Any
    we: Any
    ws: Any
    hb: Any
    ob: Any
    scl: Any
    sc: Any
    na: Any
    q: Any
    k: Any
    v: Any
    ctxt: Any
    ctx: Any
    ctx_t: Any
    lse: Any
    nb: Any
    na_t: Any
    nb_t: Any
    act: Any
    slope: Any
    psend: Any
    precv: Any
    hs: Any
    mid: Any
    ssem: Any
    rsem: Any
    zero_ssem: Any
    zero_rsem: Any
    sc_ssem: Any
    sc_rsem: Any
    xs: Any
    xr: Any
    lsem: Any


class Refs:
    def __init__(self, *groups):
        for group in groups:
            for name, ref in zip(group._fields, group):
                setattr(self, name, ref)


def split(refs, *kinds):
    out, at = [], 0
    for kind in kinds:
        size = len(kind._fields)
        out.append(kind(*refs[at : at + size]))
        at += size
    return out


class Weights(Spot):
    def __init__(self, n, rows):
        super().__init__()
        self.n = n
        self.rows = rows
        self.source = {
            TRIPLE: (n.p_whole, n.p_half), OUTPUT: (n.p_out,), EXPAND: (n.p_exp,), SHRINK: (n.p_shr,)
        }

    def view(self, kind, layer, y, z, c):
        n, r = self.n, self.rows
        if kind == EXPAND:
            return n.we.at[layer, rows_of(2 * z + y, r), rows_of(c, D)]
        at = 2 * lax.rem(z, 2) + y
        if kind == TRIPLE:
            return n.wt.at[layer, pl.ds(pl.multiple_of(HALF * c + r * at, r), r), :]
        if kind == OUTPUT:
            return n.wo.at[layer, rows_of(at, r), rows_of(c, HALF)]
        return n.ws.at[layer, rows_of(c, HALF), rows_of(2 * lax.div(z, 2) + y, 4 * r)]

    def piece(self, kind, layer, number, to):
        n, r = self.n, self.rows
        x, c = lax.div(to, 2), lax.rem(to, 2)
        if kind == TRIPLE:
            start = pl.ds(pl.multiple_of(HALF * c + r * (2 * self.odd + self.y), r), r)
            return (n.wt.at[layer, start, rows_of(x + self.core_of(number), HALF)], n.hb.at[layer, self.core_of(number)])
        if kind == OUTPUT:
            return n.ob.at[layer, number]
        if kind == EXPAND:
            return self.view(kind, layer, self.y, self.z, c)
        rows = pl.ds(pl.multiple_of(HALF * c + 192 * number, 192), 192)
        return n.ws.at[layer, rows, rows_of(2 * self.upper + self.y, 4 * r)]

    @staticmethod
    def core_of(number):
        return lax.rem(number, 2)

    def landing(self, kind, layer, number, part, to):
        spot = self.piece(kind, layer, number, to)
        return spot[part] if kind == TRIPLE else spot

    def zero_copy(self, kind, layer, number, part, to):
        return pltpu.make_async_remote_copy(
            src_ref=self.source[kind][part].at[layer],
            dst_ref=self.landing(kind, layer, number, part, to),
            send_sem=self.n.zero_ssem.at[layer, kind, part],
            recv_sem=self.n.zero_rsem.at[layer, kind, number],
            device_id=(self.d, to),
            device_id_type=MESH,
        )

    def zero_here(self, kind, layer, number, part, to):
        return pltpu.make_async_copy(
            self.source[kind][part].at[layer], self.landing(kind, layer, number, part, to),
            self.n.zero_rsem.at[layer, kind, number],
        )

    def zero(self, kind, layer):
        for number, part, to in self.targets(kind):
            away = to != self.s
            place = (kind, layer, number, part, to)
            pl.when(away)(lambda place=place: self.zero_copy(*place).start())
            pl.when(jnp.logical_not(away))(lambda place=place: self.zero_here(*place).start())

    def remote(self, ref, kind, layer, stage, sent, slot, to):
        return pltpu.make_async_remote_copy(
            src_ref=ref,
            dst_ref=ref,
            send_sem=self.n.ssem.at[layer, kind, stage, sent],
            recv_sem=self.n.rsem.at[layer, kind, stage, slot],
            device_id=to,
            device_id_type=MESH,
        )

    def spread(self, kind, layer):
        def act():
            for number, _ in self.naturals(kind):
                part = 1 if kind == TRIPLE and number >= 2 else 0
                ref = self.landing(kind, layer, number, part, self.s)
                pltpu.make_async_remote_copy(
                    src_ref=ref, dst_ref=ref, send_sem=self.n.zero_ssem.at[layer, kind, part],
                    recv_sem=self.n.zero_rsem.at[layer, kind, number], device_id=(self.d, self.peer),
                    device_id_type=MESH,
                ).wait_recv()
            n, r = self.n, self.rows
            if kind == TRIPLE:
                start = HALF * self.c + r * (2 * self.odd + self.y)
                join(n.hb[layer, 0], n.hb[layer, 1], n.wt, layer, start, 2 * (1 - self.x) * HALF, r)
            elif kind == OUTPUT:
                join(n.ob[layer, 0], n.ob[layer, 1], n.wo, layer, r * (2 * self.odd + self.y), HALF * self.c, r)
            ref = self.view(kind, layer, self.y, self.z, self.c)
            slot = self.own_slot(kind)
            for k in range(1, ZS):
                other = lax.rem(self.z + k, ZS)
                self.remote(ref, kind, layer, 0, k, slot, (2 * other + self.y, self.s)).start()
            self.remote(ref, kind, layer, 1, slot, slot, (self.across, self.s)).start()

        self.if_owner(kind, act)

    def onward(self, kind, layer, j):
        z = self.origin(kind, j)

        @pl.when(z != self.z)
        def _():
            ref = self.view(kind, layer, self.y, z, self.c)
            self.remote(ref, kind, layer, 0, 0, j, (self.across, self.s)).wait_recv()
            self.remote(ref, kind, layer, 1, j, j, (self.across, self.s)).start()

    def onward_all(self, kind, layer):
        for j in range(self.count(kind)):
            self.onward(kind, layer, j)

    def arrive(self, kind, layer):
        for j in range(self.count(kind)):
            ref = self.view(kind, layer, 1 - self.y, self.origin(kind, j), self.c)
            self.remote(ref, kind, layer, 1, j, j, (self.across, self.s)).wait_recv()

    def finish(self, kind, layer):
        for number, part, to in self.targets(kind):
            place = (kind, layer, number, part, to)
            pl.when(to != self.s)(lambda place=place: self.zero_copy(*place).wait_send())

        def act():
            ref = self.view(kind, layer, self.y, self.z, self.c)
            for k in range(1, ZS):
                self.remote(ref, kind, layer, 0, k, 0, (self.across, self.s)).wait_send()

        self.if_owner(kind, act)
        for j in range(self.count(kind)):
            ref = self.view(kind, layer, self.y, self.origin(kind, j), self.c)
            self.remote(ref, kind, layer, 1, j, j, (self.across, self.s)).wait_send()


def join(first, second, into, layer, row, col, rows):
    half = rows // 2
    top, bottom = join_packed(first[rows:], second[rows:])
    all_rows = pl.ds(pl.multiple_of(row, half), rows)
    into[layer, all_rows, pl.ds(pl.multiple_of(col, 128), 128)] = first[:rows]
    middle = pl.ds(pl.multiple_of(col + 128, 128), 128)
    into[layer, pl.ds(pl.multiple_of(row, half), half), middle] = top
    into[layer, pl.ds(pl.multiple_of(row + half, half), half), middle] = bottom
    into[layer, all_rows, pl.ds(pl.multiple_of(col + 256, 128), 128)] = second[:rows]


def greet_all(w):
    barrier = pltpu.get_barrier_semaphore()

    def one(i, carry):
        z, s = lax.div(i, SEQ), lax.rem(i, SEQ)
        away = jnp.logical_or(z != w.z, s != w.s)

        @pl.when(away)
        def _():
            pl.semaphore_signal(barrier, inc=1, device_id=(2 * z + w.y, s), device_id_type=MESH)

        return carry

    lax.fori_loop(0, w.zs * SEQ, one, 0)
    pl.semaphore_signal(barrier, inc=1, device_id=(w.across, w.s), device_id_type=MESH)
    pl.semaphore_wait(barrier, w.zs * SEQ)


def left_half(shape):
    return lax.broadcasted_iota(jnp.int32, shape, 1) < HD


def join_packed(first, second):
    first, second = first.astype(F32), second.astype(F32)
    left = left_half(first.shape)
    top = jnp.where(left, first, second)
    bottom = pltpu.roll(jnp.where(left, second, first), HD, 1)
    return top.astype(BF), bottom.astype(BF)


def pack_wide(value):
    half = value.shape[0] // 2
    top, bottom = value[:half, 128:256], pltpu.roll(value[half:, 128:256], HD, 1)
    left = left_half(top.shape)
    first, second = jnp.where(left, top, bottom), jnp.where(left, bottom, top)
    return (
        jnp.concatenate([value[:, :128], first], axis=0),
        jnp.concatenate([value[:, 256:], second], axis=0),
    )


def gather_scales_start(w):
    n = w.n
    mine = n.scl.at[w.y, w.z, w.s]
    mine[...] = n.sc_own[...]

    def one(i, carry):
        z, s = lax.div(i, SEQ), lax.rem(i, SEQ)

        @pl.when(jnp.logical_or(z != w.z, s != w.s))
        def _():
            pltpu.make_async_remote_copy(
                src_ref=mine, dst_ref=mine, send_sem=n.sc_ssem.at[i],
                recv_sem=n.sc_rsem.at[w.z * SEQ + w.s], device_id=(2 * z + w.y, s), device_id_type=MESH,
            ).start()

        return carry

    lax.fori_loop(0, w.zs * SEQ, one, 0)


def gather_scales_end(w):
    n = w.n

    def one(i, carry):
        z, s = lax.div(i, SEQ), lax.rem(i, SEQ)

        @pl.when(jnp.logical_or(z != w.z, s != w.s))
        def _():
            slot = n.scl.at[w.y, z, s]
            copy = pltpu.make_async_remote_copy(
                src_ref=slot, dst_ref=slot, send_sem=n.sc_ssem.at[i], recv_sem=n.sc_rsem.at[i],
                device_id=(2 * z + w.y, s), device_id_type=MESH,
            )
            copy.wait_recv()
            copy.wait_send()

        return carry

    lax.fori_loop(0, w.zs * SEQ, one, 0)
    count = w.zs * SEQ
    plane = n.scl.at[w.y]
    copy = pltpu.make_async_remote_copy(
        src_ref=plane, dst_ref=plane, send_sem=n.sc_ssem.at[count], recv_sem=n.sc_rsem.at[count],
        device_id=(w.across, w.s), device_id_type=MESH,
    )
    copy.start()
    copy.wait()
    wide = n.sc.shape[-1] // (2 * w.zs)
    for s in range(SEQ):
        both = [n.scl[d % 2, d // 2, s][:, :wide] for d in range(2 * w.zs)]
        rows = jnp.concatenate(both, axis=1)
        for layer in range(LAYERS):
            n.sc[layer, s : s + 1, :] = rows[layer : layer + 1, :]


def fwd_kernel(dp, *refs):
    ins, outs, saved0, saved1, scratch = split(refs, ForwardIn, ForwardHead, Saved, Saved, ForwardScratch)
    n = Refs(ins, outs, scratch)
    saved = (saved0, saved1)
    rows = n.p_exp.shape[1]
    t = n.h0.shape[0]
    w = Weights(n, rows)
    x, c, peer, sib = w.x, w.c, w.peer, w.sib
    y = 1 - x
    copies = Copies(n.lsem, n.xs, n.xr, w.d)
    waits = []

    def save(src, dst):
        waits.append(copies.local(src, dst))

    greet_all(w)
    w.zero(TRIPLE, 0)
    gather_scales_start(w)
    for kind in (OUTPUT, EXPAND, SHRINK):
        w.zero(kind, 0)
    w.spread(TRIPLE, 0)
    w.spread(OUTPUT, 0)
    n.hs[0] = n.h0[...]
    xhat, _ = norm_stats(n.hs[0])
    gather_scales_end(w)

    def share_tri(layer):
        own = n.wt.at[layer, rows_of(c, HALF), :]
        return copies.push(own, own, sib)

    def share_out(layer):
        own = n.wo.at[layer, :, rows_of(c, HALF)]
        return copies.push(own, own, sib)

    def share_shr(layer):
        own = n.ws.at[layer, rows_of(c, HALF), :]
        return copies.push(own, own, sib)

    def share_exp(layer):
        own = n.we.at[layer, :, rows_of(c, D)]
        return copies.push(own, own, sib)

    for layer in range(LAYERS):
        last = layer == LAYERS - 1
        if layer:
            xhat, _ = norm_stats(n.hs[layer])
        n.na[layer, x] = (xhat * n.sc[layer, 0:1, :] + n.sc[layer, 1:2, :]).astype(BF)
        na_sent = copies.push(n.na.at[layer, x], n.na.at[layer, x], peer)
        if layer == 0:
            w.onward_all(TRIPLE, 0)
            w.spread(EXPAND, 0)
            w.spread(SHRINK, 0)
            w.onward_all(OUTPUT, 0)
            for kind in KINDS:
                w.zero(kind, 1)
            w.arrive(TRIPLE, 0)
            tri_sent = share_tri(0)
        tri_sent.wait()

        def project(block):
            cosine, sine = n.cs[block, :, 0:128], n.cs[block, :, 128:256]
            for j in range(9):
                part = nn(n.na[layer, block], n.wt[layer, :, 128 * j : 128 * j + 128])
                lanes = pl.ds(128 * (j % 3), 128)
                if j < 3:
                    n.q[layer, block, :, lanes] = (turn(part, cosine, sine) * HD**-0.5).astype(BF)
                elif j < 6:
                    n.k[layer, block, rows_of(c, t), lanes] = turn(part, cosine, sine).astype(BF)
                else:
                    n.v[layer, block, rows_of(c, t), lanes] = part.astype(BF)

        def share(block):
            at = (layer, block, rows_of(c, t))
            return [
                copies.push(n.k.at[at], n.k.at[at], sib),
                copies.push(n.v.at[at], n.v.at[at], sib),
            ]

        project(x)
        shared = share(x)
        na_sent.wait()
        project(y)
        shared += share(y)
        w.arrive(OUTPUT, layer)
        out_sent = share_out(layer)
        for copy in shared:
            copy.wait()
        save(n.q.at[layer], saved[layer].q)
        save(n.k.at[layer], saved[layer].k)
        save(n.v.at[layer], saved[layer].v)

        def attend(block, pump):
            other = 1 - block

            def pair_step(p, carry):
                pump(p)
                lanes = pl.ds(pl.multiple_of(p * 128, 128), 128)
                q_pair = n.q[layer, block, :, lanes]
                k_same, k_cross = n.k[layer, block, :, lanes], n.k[layer, other, :, lanes]
                v_same, v_cross = n.v[layer, block, :, lanes], n.v[layer, other, :, lanes]
                for which in range(2):
                    q_head = half_of(q_pair, which)
                    s_same = nt(k_same, q_head)
                    s_cross = nt(k_cross, q_head) + n.bias[0]
                    top = jnp.maximum(
                        jnp.max(s_same, axis=0, keepdims=True), jnp.max(s_cross, axis=0, keepdims=True)
                    )
                    e_same = jnp.exp(s_same - top)
                    e_cross = jnp.exp(s_cross - top)
                    total = jnp.sum(e_same, axis=0, keepdims=True) + jnp.sum(
                        e_cross, axis=0, keepdims=True
                    )
                    mixed = tn(v_same, e_same.astype(BF)) + tn(v_cross, e_cross.astype(BF))
                    head = pl.ds(pl.multiple_of(p * 128 + which * HD, HD), HD)
                    n.ctxt[head, :] = mixed[which * HD : which * HD + HD, :] / total
                    n.lse[layer, block, pl.ds(2 * p + which, 1), :] = top + jnp.log(total)
                return carry

            lax.fori_loop(0, HALF // 128, pair_step, 0)
            n.ctx_t[layer, :, rows_of(block, t)] = n.ctxt[...].astype(BF)
            n.ctx[layer, block] = n.ctxt[...].T.astype(BF)

        def early(p):
            kind = SHRINK if layer else EXPAND
            pl.when(p > 0)(lambda: w.onward(kind, layer, p - 1))

        attend(y, early)
        out_sent.wait()
        use = 2 * layer
        n.psend[use] = nn(n.ctx[layer, y], n.wo[layer]).astype(BF)
        part_sent = copies.push(n.psend.at[use], n.precv.at[use], peer)

        if not last:
            w.spread(TRIPLE, layer + 1)
            w.spread(OUTPUT, layer + 1)

        def late(p):
            if layer == 0:
                pl.when(p == 0)(lambda: w.onward(EXPAND, layer, 2))
                pl.when(p == 0)(lambda: w.onward(EXPAND, layer, 3))
                pl.when(p > 0)(lambda: w.onward(SHRINK, layer, p - 1))

        attend(x, late)
        if not last:
            w.spread(EXPAND, layer + 1)
            w.spread(SHRINK, layer + 1)
        n.mid[layer] = n.hs[layer] + nn(n.ctx[layer, x], n.wo[layer])
        save(n.ctx.at[layer], saved[layer].ctx)
        save(n.lse.at[layer], saved[layer].lse)
        save(n.wt.at[layer], saved[layer].wt)
        save(n.wo.at[layer], saved[layer].wo)
        save(n.ctx_t.at[layer], saved[layer].ctx_t)
        for block in range(2):
            n.na_t[layer, :, block * t : block * t + t] = n.na[layer, block].T
        save(n.na_t.at[layer], saved[layer].na)
        part_sent.wait()
        n.mid[layer] = n.mid[layer] + n.precv[use].astype(F32)
        save(n.mid.at[layer], (n.mid_o0, n.mid_o1)[layer])

        xhat, _ = norm_stats(n.mid[layer])
        n.nb[layer, x] = (xhat * n.sc[layer, 2:3, :] + n.sc[layer, 3:4, :]).astype(BF)
        nb_sent = copies.push(n.nb.at[layer, x], n.nb.at[layer, x], peer)
        w.arrive(EXPAND, layer)
        exp_sent = share_exp(layer)
        w.arrive(SHRINK, layer)
        shr_sent = share_shr(layer)
        exp_sent.wait()

        def feed(block, pump):
            def step(i, carry):
                pump(i)
                lanes = pl.ds(pl.multiple_of(i * 256, 256), 256)
                value, rate = gelu_parts(nn(n.nb[layer, block], n.we[layer, :, lanes]))
                n.act[layer, block, :, lanes] = value.astype(BF)
                n.slope[layer, block, :, lanes] = rate.astype(BF)
                return carry

            lax.fori_loop(0, HID // 256, step, 0)

        def pump(i):
            if not last:

                @pl.when(i < 2)
                def _():
                    w.onward(TRIPLE, layer + 1, i)
                    w.onward(OUTPUT, layer + 1, i)

        feed(x, lambda i: None)
        shr_sent.wait()
        n.hs[layer + 1] = n.mid[layer] + nt(n.act[layer, x], n.ws[layer])
        nb_sent.wait()
        feed(y, pump)
        use = 2 * layer + 1
        n.psend[use] = nt(n.act[layer, y], n.ws[layer]).astype(BF)
        part_sent = copies.push(n.psend.at[use], n.precv.at[use], peer)
        for block in range(2):
            n.nb_t[layer, :, block * t : block * t + t] = n.nb[layer, block].T
        save(n.nb_t.at[layer], saved[layer].nb)
        save(n.act.at[layer], saved[layer].act)
        save(n.slope.at[layer], saved[layer].slope)
        save(n.we.at[layer], saved[layer].we)
        save(n.ws.at[layer], saved[layer].ws)
        if not last:
            w.onward_all(EXPAND, layer + 1)
            w.arrive(TRIPLE, layer + 1)
            tri_sent = share_tri(layer + 1)
        part_sent.wait()
        n.hs[layer + 1] = n.hs[layer + 1] + n.precv[use].astype(F32)

    n.h_out[...] = n.hs[LAYERS]
    n.sc_o[...] = n.sc[...]
    save(n.hs.at[1], n.h_mid)
    for copy in waits:
        copy.wait()
    for layer in range(LAYERS):
        for kind in KINDS:
            w.finish(kind, layer)


def forward_all(dp, h, sc_own, tables, bias, pieces):
    t = h.shape[0]
    zs, packed = dp // 2, 3 * (D // dp) // 2
    per_layer = [
        sds((D, 2 * t), BF), sds((2, t, HALF), BF), sds((2, 2 * t, HALF), BF), sds((2, 2 * t, HALF), BF),
        sds((2, t, HALF), BF), sds((HALF, 2 * t), BF), sds((2, 8, t), F32), sds((D, 2 * t), BF), sds((2, t, HID), BF),
        sds((2, t, HID), BF), sds((D, TRI), BF), sds((HALF, D), BF), sds((D, HID), BF), sds((D, HID), BF),
    ]
    token = sds((t, D), F32)
    outs = [token, token, token, token, sds((LAYERS, 4, D), F32), *per_layer, *per_layer]
    specs = [vmem(), hbm(), hbm(), hbm(), vmem(), *([hbm()] * (2 * len(per_layer)))]
    n_layers = LAYERS
    scratch = [
        pltpu.VMEM((n_layers, D, TRI), BF), pltpu.VMEM((n_layers, HALF, D), BF),
        pltpu.VMEM((n_layers, D, HID), BF), pltpu.VMEM((n_layers, D, HID), BF),
        pltpu.VMEM((n_layers, 2, packed, 128), BF), pltpu.VMEM((n_layers, 2, packed, 128), BF),
        pltpu.VMEM((2, zs, SEQ, 8, 128), F32),
        pltpu.VMEM((n_layers, 4, D), F32), pltpu.VMEM((n_layers, 2, t, D), BF),
        pltpu.VMEM((n_layers, 2, t, HALF), BF), pltpu.VMEM((n_layers, 2, 2 * t, HALF), BF),
        pltpu.VMEM((n_layers, 2, 2 * t, HALF), BF), pltpu.VMEM((HALF, t), F32),
        pltpu.VMEM((n_layers, 2, t, HALF), BF), pltpu.VMEM((n_layers, HALF, 2 * t), BF),
        pltpu.VMEM((n_layers, 2, 8, t), F32), pltpu.VMEM((n_layers, 2, t, D), BF),
        pltpu.VMEM((n_layers, D, 2 * t), BF), pltpu.VMEM((n_layers, D, 2 * t), BF),
        pltpu.VMEM((n_layers, 2, t, HID), BF),
        pltpu.VMEM((n_layers, 2, t, HID), BF), pltpu.VMEM((2 * n_layers, t, D), BF),
        pltpu.VMEM((2 * n_layers, t, D), BF), pltpu.VMEM((n_layers + 1, t, D), F32),
        pltpu.VMEM((n_layers, t, D), F32),
        pltpu.SemaphoreType.DMA((n_layers, len(KINDS), 2, zs)),
        pltpu.SemaphoreType.DMA((n_layers, len(KINDS), 2, zs)),
        pltpu.SemaphoreType.DMA((n_layers, len(KINDS), 2)), pltpu.SemaphoreType.DMA((n_layers, len(KINDS), 4)),
        pltpu.SemaphoreType.DMA((zs * SEQ + 1,)), pltpu.SemaphoreType.DMA((zs * SEQ + 1,)),
        pltpu.SemaphoreType.DMA((24,)), pltpu.SemaphoreType.DMA((24,)), pltpu.SemaphoreType.DMA((32,)),
    ]
    results = pl.pallas_call(
        functools.partial(fwd_kernel, dp),
        name="forward",
        out_shape=outs,
        in_specs=[vmem(), vmem(), vmem(), pl.BlockSpec(memory_space=pltpu.SMEM), *([hbm()] * 5)],
        out_specs=specs,
        scratch_shapes=scratch,
        cost_estimate=pl.CostEstimate(flops=22 << 30, bytes_accessed=32 << 20, transcendentals=0),
        compiler_params=pltpu.CompilerParams(
            collective_id=4, has_side_effects=True, vmem_limit_bytes=VMEM_BYTES
        ),
    )(h, sc_own, tables, bias, *pieces)
    return split(results, ForwardHead, Saved, Saved)


def pack_rows(low, c):
    half = low.shape[1] // 2
    even = [low[:, :, :128], jnp.concatenate([low[:, :half, 128:], low[:, half:, 128:]], axis=2)]
    odd = [low[:, :, 64:], jnp.concatenate([low[:, half:, :64], low[:, :half, :64]], axis=2)]
    return jnp.where(c == 0, jnp.concatenate(even, axis=1), jnp.concatenate(odd, axis=1))


def unpack_rows(packed, c):
    rows = 2 * packed.shape[1] // 3
    wide, rest = packed[:, :rows], packed[:, rows:]
    even = jnp.concatenate([wide, jnp.concatenate([rest[:, :, :64], rest[:, :, 64:]], axis=1)], axis=2)
    odd = jnp.concatenate([jnp.concatenate([rest[:, :, 64:], rest[:, :, :64]], axis=1), wide], axis=2)
    return jnp.where(c == 0, even, odd)


def pieces_of(triple_weight, output_weight, expand_weight, shrink_weight, c):
    tri = triple_weight.astype(BF)
    whole = jnp.where(c == 0, tri[:, :, :HALF], tri[:, :, 192:])
    half = jnp.where(c == 0, tri[:, :, HALF:], tri[:, :, :192])
    shr = jnp.swapaxes(shrink_weight.astype(BF), 1, 2)
    return whole, pack_rows(half, c), pack_rows(output_weight.astype(BF), c), expand_weight.astype(BF), shr


class Sums(Spot):
    def __init__(self, n, rows):
        super().__init__()
        self.n = n
        self.rows = rows
        self.landed = {TRIPLE: n.y_tri, OUTPUT: n.y_out, EXPAND: n.y_exp, SHRINK: n.y_shr}
        self.owned = {TRIPLE: n.z_tri, OUTPUT: n.z_out, EXPAND: n.z_exp, SHRINK: n.z_shr}
        self.final = {TRIPLE: (n.f_whole, n.f_half), OUTPUT: (n.f_out,), EXPAND: (n.f_exp,), SHRINK: (n.f_shr,)}

    def view(self, kind, layer, y, z):
        n, r = self.n, self.rows
        if kind == EXPAND:
            return n.ge.at[layer, rows_of(2 * z + y, r), :]
        if kind == SHRINK:
            return n.gs.at[layer, :, rows_of(2 * lax.div(z, 2) + y, 4 * r)]
        return (n.gt if kind == TRIPLE else n.go).at[layer, rows_of(2 * lax.rem(z, 2) + y, r), :]

    def remote(self, src, dst, kind, layer, stage, sent, slot, to):
        return pltpu.make_async_remote_copy(
            src_ref=src,
            dst_ref=dst,
            send_sem=self.n.ssem.at[layer, kind, stage, sent],
            recv_sem=self.n.rsem.at[layer, kind, stage, slot],
            device_id=to,
            device_id_type=MESH,
        )

    def across_copy(self, kind, layer, j):
        return self.remote(
            self.view(kind, layer, 1 - self.y, self.origin(kind, j)), self.landed[kind].at[layer, j],
            kind, layer, 0, j, j, (self.across, self.s),
        )

    def across_all(self, kind, layer):
        for j in range(self.count(kind)):
            self.across_copy(kind, layer, j).start()

    def along_copy(self, kind, layer, j):
        z = self.origin(kind, j)
        slot = lax.rem(self.z - z + ZS - 1, ZS)
        mine = self.view(kind, layer, self.y, z)
        return self.remote(mine, self.owned[kind].at[layer, slot], kind, layer, 1, j, slot, (2 * z + self.y, self.s))

    def along(self, kind, layer, j):
        z = self.origin(kind, j)
        self.across_copy(kind, layer, j).wait_recv()
        mine = self.view(kind, layer, self.y, z)
        mine[...] = (mine[...].astype(F32) + self.landed[kind][layer, j].astype(F32)).astype(BF)
        pl.when(z != self.z)(lambda: self.along_copy(kind, layer, j).start())

    def along_all(self, kind, layer):
        for j in range(self.count(kind)):
            self.along(kind, layer, j)

    def parts(self, kind, layer):
        n = self.n
        mine = self.view(kind, layer, self.y, self.z)
        if kind == TRIPLE:
            return (
                mine.at[:, rows_of(self.x, HALF)], mine.at[:, rows_of(self.x + 1, HALF)],
                n.half_out.at[layer, 0], n.half_out.at[layer, 1],
            )
        if kind == OUTPUT:
            return n.out_out.at[layer, 0], n.out_out.at[layer, 1]
        return (mine,) if kind == EXPAND else (mine.at[pl.ds(0, 192), :], mine.at[pl.ds(192, 192), :])

    def home_copy(self, kind, layer, number, to, here=False):
        src = self.parts(kind, layer)[number]
        part = 1 if kind == TRIPLE and number >= 2 else 0
        dst = self.final[kind][part].at[layer]
        sem = self.n.home_rsem.at[layer, kind, part]
        if here:
            return pltpu.make_async_copy(src, dst, sem)
        return pltpu.make_async_remote_copy(
            src_ref=src, dst_ref=dst, send_sem=self.n.home_ssem.at[layer, kind, number], recv_sem=sem,
            device_id=(self.d, to), device_id_type=MESH,
        )

    def total(self, kind, layer):
        n = self.n

        def act():
            for slot in range(ZS - 1):
                ref = self.owned[kind].at[layer, slot]
                self.remote(ref, ref, kind, layer, 1, 0, slot, (self.across, self.s)).wait_recv()
            mine = self.view(kind, layer, self.y, self.z)
            value = mine[...].astype(F32)
            for slot in range(ZS - 1):
                value = value + self.owned[kind][layer, slot].astype(F32)
            n.squares[...] = n.squares[...] + squared(value)
            mine[...] = value.astype(BF)
            if kind == OUTPUT:
                first, second = pack_wide(value)
                n.out_out[layer, 0] = first.astype(BF)
                n.out_out[layer, 1] = second.astype(BF)
            if kind == TRIPLE:
                cut = mine[:, rows_of(2 * (1 - self.x), HALF)].astype(F32)
                first, second = pack_wide(cut)
                n.half_out[layer, 0] = first.astype(BF)
                n.half_out[layer, 1] = second.astype(BF)
            for number, to in self.naturals(kind):
                away = to != self.s
                place = (kind, layer, number, to)
                pl.when(away)(lambda place=place: self.home_copy(*place).start())
                pl.when(jnp.logical_not(away))(lambda place=place: self.home_copy(*place, True).start())

        self.if_owner(kind, act)

    def home(self, kind, layer):
        for part, final in enumerate(self.final[kind]):
            ref = final.at[layer]
            pltpu.make_async_remote_copy(
                src_ref=ref, dst_ref=ref, send_sem=self.n.home_ssem.at[layer, kind, 0],
                recv_sem=self.n.home_rsem.at[layer, kind, part], device_id=(self.d, self.peer), device_id_type=MESH,
            ).wait_recv()

    def finish(self, kind, layer):
        for j in range(self.count(kind)):
            self.across_copy(kind, layer, j).wait_send()
            pl.when(self.origin(kind, j) != self.z)(
                lambda j=j: self.along_copy(kind, layer, j).wait_send()
            )

        def act():
            for number, to in self.naturals(kind):
                place = (kind, layer, number, to)
                pl.when(to != self.s)(lambda place=place: self.home_copy(*place).wait_send())

        self.if_owner(kind, act)


def squared(value):
    return jnp.sum(jnp.sum(value * value, axis=1, keepdims=True), axis=0, keepdims=True)


def everywhere_start(w, use, buf):
    n = w.n
    mine = buf.at[w.y, w.z, w.s]

    def one(i, carry):
        z, s = lax.div(i, SEQ), lax.rem(i, SEQ)

        @pl.when(jnp.logical_or(z != w.z, s != w.s))
        def _():
            pltpu.make_async_remote_copy(
                src_ref=mine, dst_ref=mine, send_sem=n.ev_ssem.at[use, i],
                recv_sem=n.ev_rsem.at[use, w.z * SEQ + w.s], device_id=(2 * z + w.y, s), device_id_type=MESH,
            ).start()

        return carry

    lax.fori_loop(0, w.zs * SEQ, one, 0)


def everywhere_end(w, use, buf, pair):
    n = w.n

    def one(i, carry):
        z, s = lax.div(i, SEQ), lax.rem(i, SEQ)

        @pl.when(jnp.logical_or(z != w.z, s != w.s))
        def _():
            slot = buf.at[w.y, z, s]
            copy = pltpu.make_async_remote_copy(
                src_ref=slot, dst_ref=slot, send_sem=n.ev_ssem.at[use, i], recv_sem=n.ev_rsem.at[use, i],
                device_id=(2 * z + w.y, s), device_id_type=MESH,
            )
            copy.wait_recv()
            copy.wait_send()

        return carry

    lax.fori_loop(0, w.zs * SEQ, one, 0)

    def add(i, total):
        return total + buf[w.y, lax.div(i, SEQ), lax.rem(i, SEQ)]

    pair[w.y] = lax.fori_loop(1, w.zs * SEQ, add, buf[w.y, 0, 0])
    count = w.zs * SEQ
    copy = pltpu.make_async_remote_copy(
        src_ref=pair.at[w.y], dst_ref=pair.at[w.y], send_sem=n.ev_ssem.at[use, count],
        recv_sem=n.ev_rsem.at[use, count], device_id=(w.across, w.s), device_id_type=MESH,
    )
    copy.start()
    copy.wait()
    return pair[0] + pair[1]


class Loaded(NamedTuple):
    na: Any
    q: Any
    k: Any
    v: Any
    ctx: Any
    ctx_t: Any
    lse: Any
    nb: Any
    act: Any
    slope: Any
    wt: Any
    wo: Any
    we: Any
    ws: Any
    h: Any
    mid: Any


class BackwardIn(NamedTuple):
    g0: Any
    sc: Any
    cs: Any
    bias: Any


class BackwardOut(NamedTuple):
    g_out: Any
    scale_o: Any
    norm_o: Any
    whole_g: Any
    half_g: Any
    out_g: Any
    exp_g: Any
    shr_g: Any


class BackwardScratch(NamedTuple):
    gl: Any
    gl_t: Any
    hg: Any
    ml: Any
    cg: Any
    delta: Any
    dqt: Any
    dk: Any
    dv: Any
    kvsend: Any
    kvrecv: Any
    pg: Any
    part: Any
    psend: Any
    precv: Any
    gs_exp: Any
    gr_exp: Any
    gs_shr: Any
    gr_shr: Any
    gr_att: Any
    gt: Any
    go: Any
    ge: Any
    gs: Any
    y_tri: Any
    y_out: Any
    y_exp: Any
    y_shr: Any
    z_tri: Any
    z_out: Any
    z_exp: Any
    z_shr: Any
    half_out: Any
    out_out: Any
    f_whole: Any
    f_half: Any
    f_out: Any
    f_exp: Any
    f_shr: Any
    squares: Any
    early: Any
    early_pair: Any
    late: Any
    late_pair: Any
    sq: Any
    sq_pair: Any
    ssem: Any
    rsem: Any
    home_ssem: Any
    home_rsem: Any
    ev_ssem: Any
    ev_rsem: Any
    xs: Any
    xr: Any
    lsem: Any


def bwd_kernel(dp, *refs):
    ins, saved0, saved1, outs, loaded, scratch = split(
        refs, BackwardIn, Loaded, Loaded, BackwardOut, Loaded, BackwardScratch
    )
    n = Refs(ins, outs, loaded, scratch)
    saved = (saved0, saved1)
    t = n.g0.shape[0]
    w = Sums(n, D // dp)
    x, c, peer, sib = w.x, w.c, w.peer, w.sib
    y = 1 - x
    copies = Copies(n.lsem, n.xs, n.xr, w.d)
    loading = {}

    def load(layer, *wanted):
        for place in wanted:
            loading[place] = copies.local(saved[layer][place], loaded[place])

    def ready(*wanted):
        for place in wanted:
            loading[place].wait()

    na, q, k, v, ctx, ctx_t, lse, nb, act, slope, wt, wo, we, ws, h, mid = range(len(Loaded._fields))
    feed_places = (ws, slope, we, act, nb, mid)
    attend_places = (wo, ctx, q, k, v, lse, wt, na, ctx_t, h)
    load(LAYERS - 1, *feed_places, *attend_places)
    greet_all(w)
    n.g_out[...] = n.g0[...]

    for layer in reversed(range(LAYERS)):
        top = layer == LAYERS - 1

        n.gl[layer, x] = n.g_out[...].astype(BF)
        g_sent = copies.push(n.gl.at[layer, x], n.gl.at[layer, x], peer)
        ready(ws, slope, we)

        def back(block, pump):
            def step(i, carry):
                pump(i)
                lanes = pl.ds(pl.multiple_of(i * 256, 256), 256)
                pulled = nn(n.gl[layer, block], n.ws[:, lanes])
                n.hg[block, :, lanes] = (pulled * n.slope[block, :, lanes].astype(F32)).astype(BF)
                return carry

            lax.fori_loop(0, HID // 256, step, 0)
            return nt(n.hg[block], n.we[...])

        def pump_tri(i):
            if not top:

                @pl.when(i < 2)
                def _():
                    w.along(TRIPLE, layer + 1, i)
                    w.along(OUTPUT, layer + 1, i)

        n.part[...] = back(x, lambda i: None)
        g_sent.wait()
        use = 2 * layer
        n.psend[...] = back(y, lambda i: None).astype(BF)
        part_sent = copies.push(n.psend, n.precv.at[use], peer)
        ready(act, nb, mid)
        for block in range(2):
            n.gl_t[:, block * t : block * t + t] = n.gl[layer, block].T

        def exp_tile(which, i):
            off = pl.ds(pl.multiple_of(which * D + i * 256, 256), 256)
            return nn(n.nb[...], n.hg[:, :, off].reshape(2 * t, 256))

        def shr_tile(which, i):
            off = pl.ds(pl.multiple_of(i * 256, 256), 256)
            return nn(n.gl_t[rows_of(which, HALF), :], n.act[:, :, off].reshape(2 * t, 256))

        def send_exp(i, carry):
            at = pl.ds(pl.multiple_of(i * 256, 256), 256)
            n.gs_exp[:, at] = exp_tile(1 - c, i).astype(BF)
            return carry

        def send_shr(i, carry):
            at = pl.ds(pl.multiple_of(i * 256, 256), 256)
            n.gs_shr[:, at] = shr_tile(1 - c, i).astype(BF)
            return carry

        lax.fori_loop(0, D // 256, send_exp, 0)
        exp_sent = copies.push(n.gs_exp, n.gr_exp, sib)
        lax.fori_loop(0, HID // 256, send_shr, 0)
        shr_sent = copies.push(n.gs_shr, n.gr_shr, sib)

        def keep_exp(i, carry):
            at = pl.ds(pl.multiple_of(i * 256, 256), 256)
            n.ge[layer, :, at] = (exp_tile(c, i) + n.gr_exp[:, at].astype(F32)).astype(BF)
            return carry

        def keep_shr(i, carry):
            pump_tri(i)
            at = pl.ds(pl.multiple_of(i * 256, 256), 256)
            n.gs[layer, :, at] = (shr_tile(c, i) + n.gr_shr[:, at].astype(F32)).astype(BF)
            return carry

        exp_sent.wait()
        lax.fori_loop(0, D // 256, keep_exp, 0)
        w.across_all(EXPAND, layer)
        shr_sent.wait()
        lax.fori_loop(0, HID // 256, keep_shr, 0)
        w.across_all(SHRINK, layer)
        part_sent.wait()
        dy = n.part[...] + n.precv[use].astype(F32)
        back_mid, rows_b = norm_back(n.mid[...], n.sc[layer, 2:3, :], dy)
        n.g_out[...] = n.g_out[...] + back_mid

        n.ml[layer, x] = n.g_out[...].astype(BF)
        ml_sent = copies.push(n.ml.at[layer, x], n.ml.at[layer, x], peer)
        if layer:
            load(layer - 1, *feed_places)
        n.dk[...] = jnp.zeros_like(n.dk)
        n.dv[...] = jnp.zeros_like(n.dv)
        ready(wo, ctx, q, k, v, lse)

        def attend(block, pump):
            other = 1 - block
            n.cg[block] = nt(n.ml[layer, block], n.wo[...]).astype(BF)
            weighed = (n.cg[block].astype(F32) * n.ctx[block].astype(F32)).T
            for head in range(HALF // HD):
                n.delta[head : head + 1, :] = jnp.sum(
                    weighed[head * HD : head * HD + HD, :], axis=0, keepdims=True
                )

            def pair_step(p, carry):
                pump(p)
                lanes = pl.ds(pl.multiple_of(p * 128, 128), 128)
                q_pair, cg_pair = n.q[block, :, lanes], n.cg[block, :, lanes]
                for which in range(2):
                    q_head, cg_head = half_of(q_pair, which), half_of(cg_pair, which)
                    row = pl.ds(2 * p + which, 1)
                    total, dots = n.lse[block, row, :], n.delta[row, :]
                    turned = None
                    for side in (block, other):
                        k_pair, v_pair = n.k[side, :, lanes], n.v[side, :, lanes]
                        scores = nt(k_pair, q_head)
                        if side is other:
                            scores = scores + n.bias[0]
                        probs = jnp.exp(scores - total)
                        score_grad = (probs * (nt(v_pair, cg_head) - dots)).astype(BF)
                        n.dv[side, :, lanes] += nn(probs.astype(BF), cg_head)
                        n.dk[side, :, lanes] += nn(score_grad, q_head)
                        piece = tn(k_pair, score_grad)
                        turned = piece if turned is None else turned + piece
                    head = pl.ds(pl.multiple_of(p * 128 + which * HD, HD), HD)
                    n.dqt[block, head, :] = turned[which * HD : which * HD + HD, :] * HD**-0.5
                return carry

            lax.fori_loop(0, HALF // 128, pair_step, 0)

        attend(x, lambda p: None)
        ml_sent.wait()
        attend(y, lambda p: w.along(EXPAND, layer, p))
        theirs, mine = rows_of(1 - c, t), rows_of(c, t)
        for side in range(2):
            n.kvsend[side, :, pl.ds(0, HALF)] = n.dk[side, theirs, :].astype(BF)
            n.kvsend[side, :, pl.ds(HALF, HALF)] = n.dv[side, theirs, :].astype(BF)
        kv_sent = copies.push(n.kvsend, n.kvrecv.at[layer], sib)
        w.along(EXPAND, layer, 3)

        def unturn(block, j, value):
            cosine, sine = n.cs[block, :, 0:128], n.cs[block, :, 128:256]
            rounded = value.astype(BF).astype(F32)
            n.pg[block, :, pl.ds(128 * j, 128)] = turn(rounded, cosine, -sine).astype(BF)

        for side in range(2):
            for j in range(3):
                unturn(side, j, n.dqt[side, 128 * j : 128 * j + 128, :].T)
        kv_sent.wait()
        for side in range(2):
            for j in range(3):
                at = pl.ds(128 * j, 128)
                unturn(side, 3 + j, n.dk[side, mine, at] + n.kvrecv[layer, side, :, at].astype(F32))
                n.pg[side, :, pl.ds(D + 128 * j, 128)] = (
                    n.dv[side, mine, at] + n.kvrecv[layer, side, :, pl.ds(HALF + 128 * j, 128)].astype(F32)
                ).astype(BF)
        ready(wt, na, ctx_t, h)
        use = 2 * layer + 1
        n.psend[...] = nt(n.pg[y], n.wt[...]).astype(BF)
        part_sent = copies.push(n.psend, n.precv.at[use], peer)
        rows = D // dp

        def send_tri(i, carry):
            pl.when(i < 2)(lambda: w.along(SHRINK, layer, i))
            off = pl.ds(pl.multiple_of((1 - c) * HALF + i * rows, rows), rows)
            n.gs_shr[rows_of(i, rows), pl.ds(0, TRI)] = nn(n.na[off, :], n.pg[...].reshape(2 * t, TRI)).astype(BF)
            return carry

        lax.fori_loop(0, w.zs, send_tri, 0)
        tri_cols, out_cols = pl.ds(0, TRI), pl.ds(TRI, HALF)
        tri_sent = copies.push(n.gs_shr.at[:, tri_cols], n.gr_att.at[:, tri_cols], sib)
        theirs_too = n.ml[layer, :, :, rows_of(1 - c, HALF)].reshape(2 * t, HALF)
        n.gs_shr[:, out_cols] = nn(n.ctx_t[...], theirs_too).astype(BF)
        out_sent = copies.push(n.gs_shr.at[:, out_cols], n.gr_att.at[:, out_cols], sib)
        n.part[...] = nt(n.pg[x], n.wt[...])
        tri_sent.wait()

        def keep_tri(i, carry):
            at = rows_of(i, rows)
            row_block = n.na[pl.ds(pl.multiple_of(c * HALF + i * rows, rows), rows), :]
            value = nn(row_block, n.pg[...].reshape(2 * t, TRI)) + n.gr_att[at, tri_cols].astype(F32)
            n.gt[layer, at, :] = value.astype(BF)
            return carry

        lax.fori_loop(0, w.zs, keep_tri, 0)
        w.across_all(TRIPLE, layer)
        out_sent.wait()
        mine_too = n.ml[layer, :, :, rows_of(c, HALF)].reshape(2 * t, HALF)
        value = nn(n.ctx_t[...], mine_too) + n.gr_att[:, out_cols].astype(F32)
        n.go[layer] = value.astype(BF)
        w.across_all(OUTPUT, layer)
        part_sent.wait()
        dy = n.part[...] + n.precv[use].astype(F32)
        back_h, rows_a = norm_back(n.h[...], n.sc[layer, 0:1, :], dy)
        n.g_out[...] = n.g_out[...] + back_h
        mine_at = (w.y, w.z, w.s)
        if layer:
            load(layer - 1, *attend_places)
            n.early[(*mine_at, pl.ds(0, 2))] = rows_a
            n.early[(*mine_at, pl.ds(2, 2))] = rows_b
        else:
            n.early[(*mine_at, pl.ds(4, 2))] = rows_b
            n.late[mine_at] = rows_a

    everywhere_start(w, 0, n.early)
    everywhere_start(w, 1, n.late)
    n.squares[...] = jnp.zeros_like(n.squares)
    for kind in (EXPAND, SHRINK, TRIPLE, OUTPUT):
        w.total(kind, 1)
    w.along_all(TRIPLE, 0)
    w.along_all(OUTPUT, 0)
    for kind in (EXPAND, SHRINK):
        w.total(kind, 0)
    first = everywhere_end(w, 0, n.early, n.early_pair)
    second = everywhere_end(w, 1, n.late, n.late_pair)
    n.scale_o[1, pl.ds(0, 2)] = first[0:2]
    n.scale_o[1, pl.ds(2, 2)] = first[2:4]
    n.scale_o[0, pl.ds(0, 2)] = second
    n.scale_o[0, pl.ds(2, 2)] = first[4:6]
    for kind in (TRIPLE, OUTPUT):
        w.total(kind, 0)
    n.sq[w.y, w.z, w.s] = jnp.broadcast_to(n.squares[...], (8, 128))
    everywhere_start(w, 2, n.sq)
    for layer in range(LAYERS):
        for kind in KINDS:
            w.home(kind, layer)
    outputs = [
        copies.local(a, b)
        for a, b in (
            (n.f_whole, n.whole_g), (n.f_half, n.half_g), (n.f_out, n.out_g), (n.f_exp, n.exp_g), (n.f_shr, n.shr_g)
        )
    ]
    total = everywhere_end(w, 2, n.sq, n.sq_pair)
    n.norm_o[...] = total + squared(first[0:6]) + squared(second)
    for copy in outputs:
        copy.wait()
    for layer in range(LAYERS):
        for kind in KINDS:
            w.finish(kind, layer)


def backward_all(dp, g, f, residual, tables, bias):
    t = g.shape[0]
    zs = dp // 2
    r = D // dp
    packed = 3 * r // 2
    head, saved0, saved1 = f
    saved = (*saved0, residual, head.mid_o0, *saved1, head.h_mid, head.mid_o1)
    outs = [
        sds((t, D), F32), sds((LAYERS, 4, D), F32), sds((8, 128), F32), sds((LAYERS, r, HALF), BF),
        sds((LAYERS, packed, 128), BF), sds((LAYERS, packed, 128), BF), sds((LAYERS, r, D), BF),
        sds((LAYERS, 192, 4 * r), BF),
    ]
    v = pltpu.VMEM
    ll = LAYERS
    scratch = [
        *(v(array.shape, array.dtype) for array in saved[: len(Loaded._fields)]),
        v((ll, 2, t, D), BF), v((D, 2 * t), BF), v((2, t, HID), BF), v((ll, 2, t, D), BF), v((2, t, HALF), BF), v((8, t), F32),
        v((2, HALF, t), F32), v((2, 2 * t, HALF), F32), v((2, 2 * t, HALF), F32), v((2, t, D), BF),
        v((ll, 2, t, D), BF), v((2, t, TRI), BF), v((t, D), F32), v((t, D), BF), v((2 * ll, t, D), BF),
        v((D, D), BF), v((D, D), BF), v((HALF, HID), BF), v((HALF, HID), BF), v((HALF, HID), BF),
        v((ll, HALF, TRI), BF), v((ll, HALF, HALF), BF), v((ll, D, D), BF), v((ll, HALF, HID), BF),
        v((ll, 2, r, TRI), BF), v((ll, 2, r, HALF), BF), v((ll, 4, r, D), BF), v((ll, 2, HALF, 4 * r), BF),
        v((ll, 3, r, TRI), BF), v((ll, 3, r, HALF), BF), v((ll, 3, r, D), BF), v((ll, 3, HALF, 4 * r), BF),
        v((ll, 2, packed, 128), BF), v((ll, 2, packed, 128), BF),
        v((ll, r, HALF), BF), v((ll, packed, 128), BF), v((ll, packed, 128), BF), v((ll, r, D), BF),
        v((ll, 192, 4 * r), BF), v((1, 1), F32),
        v((2, zs, SEQ, 8, D), F32), v((2, 8, D), F32), v((2, zs, SEQ, 2, D), F32), v((2, 2, D), F32),
        v((2, zs, SEQ, 8, 128), F32), v((2, 8, 128), F32),
        pltpu.SemaphoreType.DMA((ll, len(KINDS), 2, zs)), pltpu.SemaphoreType.DMA((ll, len(KINDS), 2, zs)),
        pltpu.SemaphoreType.DMA((ll, len(KINDS), 4)), pltpu.SemaphoreType.DMA((ll, len(KINDS), 2)),
        pltpu.SemaphoreType.DMA((3, zs * SEQ + 1)), pltpu.SemaphoreType.DMA((3, zs * SEQ + 1)),
        pltpu.SemaphoreType.DMA((20,)), pltpu.SemaphoreType.DMA((20,)), pltpu.SemaphoreType.DMA((40,)),
    ]
    results = pl.pallas_call(
        functools.partial(bwd_kernel, dp),
        name="backward",
        out_shape=outs,
        in_specs=[vmem(), vmem(), vmem(), pl.BlockSpec(memory_space=pltpu.SMEM), *([hbm()] * len(saved))],
        out_specs=[vmem()] * 3 + [hbm()] * 5,
        scratch_shapes=scratch,
        cost_estimate=pl.CostEstimate(flops=44 << 30, bytes_accessed=48 << 20, transcendentals=0),
        compiler_params=pltpu.CompilerParams(
            collective_id=5, has_side_effects=True, vmem_limit_bytes=VMEM_BYTES
        ),
    )(g, head.sc_o, tables, bias, *saved)
    return BackwardOut(*results)


class Moves:
    def __init__(self, dp):
        self.dp = dp
        self.d = lax.axis_index("dp")
        s = lax.axis_index("seq")
        self.s, self.x, self.c = s, s // 2, s % 2
        half = dp // 2
        ids = [(d, s) for d in range(dp) for s in range(SEQ)]
        self.tri = []
        for r in range(2):
            for j in range(3):
                perm = []
                for d, s in ids:
                    b = (3 * s + j) % 4
                    to = (2 * (d % half) + (r ^ (b % 2)), 2 * (b // 2) + d // half)
                    perm.append((d * SEQ + s, to[0] * SEQ + to[1]))
                self.tri.append(perm)
        self.out = []
        for r in range(2):
            perm = []
            for d, s in ids:
                to = (2 * (d % half) + (r ^ (s % 2)), 2 * (d // half) + s // 2)
                perm.append((d * SEQ + s, to[0] * SEQ + to[1]))
            self.out.append(perm)
        self.shr = []
        for k in range(4):
            perm = []
            for d, s in ids:
                to = (4 * (d % (dp // 4)) + (k + s) % 4, d // (dp // 4))
                perm.append((d * SEQ + s, to[0] * SEQ + to[1]))
            self.shr.append(perm)

    def send(self, piece, perm, back):
        if back:
            perm = [(b, a) for a, b in perm]
        return lax.ppermute(piece, ("dp", "seq"), perm)

    @staticmethod
    def pick(pieces, index):
        return lax.dynamic_index_in_dim(jnp.stack(pieces), index, 0, keepdims=False)

    def tri_out(self, low):
        n, rows, _ = low.shape
        halves = low.reshape(n, 2, rows // 2, 3, 192)
        got = []
        for r in range(2):
            for j in range(3):
                which = r ^ (((3 * self.s + j) % 4) % 2)
                piece = lax.dynamic_index_in_dim(halves[:, :, :, j], which, 1, keepdims=False)
                got.append(self.send(piece, self.tri[3 * r + j], False))
        parts = []
        for t in range(3):
            for bb in range(2):
                r, j = bb ^ (self.d % 2), (t + 2 * self.x + bb) % 3
                parts.append(self.pick(got, 3 * r + j))
        return jnp.concatenate(parts, axis=-1)

    def tri_back(self, grad):
        n, rows, _ = grad.shape
        got = []
        for r in range(2):
            for j in range(3):
                bb = (self.d % 2) ^ r
                t = (j - (2 * self.x + bb)) % 3
                piece = lax.dynamic_slice_in_dim(grad, (2 * t + bb) * 192, 192, 2)
                got.append(self.send(piece, self.tri[3 * r + j], True))
        cols = []
        for j in range(3):
            two = []
            for hh in range(2):
                r = hh ^ (((3 * self.s + j) % 4) % 2)
                two.append(self.pick([got[j], got[3 + j]], r))
            cols.append(jnp.concatenate(two, axis=1))
        return jnp.concatenate(cols, axis=-1)

    def out_out(self, low):
        n, rows, _ = low.shape
        halves = low.reshape(n, 2, rows // 2, 192)
        got = [
            self.send(
                lax.dynamic_index_in_dim(halves, r ^ (self.s % 2), 1, keepdims=False), self.out[r], False
            )
            for r in range(2)
        ]
        return jnp.concatenate([self.pick(got, u ^ (self.d % 2)) for u in range(2)], axis=-1)

    def out_back(self, grad):
        got = []
        for r in range(2):
            u = r ^ (self.d % 2)
            got.append(self.send(lax.dynamic_slice_in_dim(grad, u * 192, 192, 2), self.out[r], True))
        return jnp.concatenate([self.pick(got, hh ^ (self.s % 2)) for hh in range(2)], axis=1)

    def shr_out(self, low):
        n, rows, _ = low.shape
        subs = low.reshape(n, 4, rows // 4, 192)
        got = [
            self.send(
                lax.dynamic_index_in_dim(subs, (k + self.s) % 4, 1, keepdims=False), self.shr[k], False
            )
            for k in range(4)
        ]
        return jnp.concatenate([self.pick(got, (self.d - s) % 4) for s in range(4)], axis=-1)

    def shr_back(self, grad):
        got = []
        for k in range(4):
            piece = lax.dynamic_slice_in_dim(grad, ((self.d - k) % 4) * 192, 192, 2)
            got.append(self.send(piece, self.shr[k], True))
        return jnp.concatenate([self.pick(got, (sub - self.s) % 4) for sub in range(4)], axis=1)


def tables_here(segments, t, x, c):
    group = segments.shape[0]
    whole = segments[0] == segments[group - 1]
    place_in_half = c * t + jnp.arange(t, dtype=jnp.int32)
    second = jnp.where(whole, group // 2, 0).astype(jnp.int32)
    positions = jnp.stack([place_in_half, place_in_half + second]).astype(F32)
    lane = jnp.arange(128, dtype=jnp.int32)
    inverse = 1.0 / ROTARY_BASE ** ((lane % (HD // 2)).astype(F32) * (2.0 / HD))
    angles = positions[:, :, None] * inverse[None, None, :]
    sign = jnp.where(lane % HD < HD // 2, -1.0, 1.0).astype(F32)
    tables = jnp.concatenate([jnp.cos(angles), jnp.sin(angles) * sign], axis=-1)
    bias = jnp.where(whole, 0.0, MASKED).astype(F32).reshape(1)
    return tables, bias


def layers_narrow(
    dp, moves, residual, cotangent, scales_weight, tables, bias,
    triple_weight, output_weight, expand_weight, shrink_weight,
):
    d, s = lax.axis_index("dp"), lax.axis_index("seq")
    scales_all = lax.psum(
        lax.dynamic_update_slice(
            jnp.zeros((LAYERS, 4, D), F32), scales_weight.astype(BF).astype(F32), (0, s, d * (D // dp))
        ),
        ("dp", "seq"),
    )
    tri = moves.tri_out(triple_weight.astype(BF))
    out = moves.out_out(output_weight.astype(BF))
    shr = moves.shr_out(shrink_weight.astype(BF))
    attend_parts = jnp.concatenate([tri, out], axis=-1)
    feed_parts = jnp.concatenate([expand_weight.astype(BF), shr], axis=-1)
    gather = functools.partial(lax.all_gather, axis_name="dp", axis=0, tiled=True)
    wa, wf = [], []
    for layer in range(LAYERS):
        wa.append(gather(attend_parts[layer]))
        wf.append(gather(feed_parts[layer]))

    stream = residual
    kept = []
    for layer in range(LAYERS):
        scales = scales_all[layer]
        middle, *attend_saved = attend_fwd(stream, wa[layer], scales, tables, bias)
        following, *feed_saved = feed_fwd(middle, wf[layer], scales)
        kept.append((stream, middle, attend_saved, feed_saved))
        stream = following

    g = cotangent
    attend_grads, feed_grads, scale_grads = [None] * LAYERS, [None] * LAYERS, [None] * LAYERS
    scatter = functools.partial(lax.psum_scatter, axis_name="dp", scatter_dimension=0, tiled=True)
    for layer in reversed(range(LAYERS)):
        scales = scales_all[layer]
        h, middle, attend_saved, feed_saved = kept[layer]
        mg, feed_grad, rows_b = feed_bwd(g, middle, wf[layer], scales, *feed_saved)
        feed_grads[layer] = scatter(feed_grad).astype(F32)
        g, attend_grad, rows_a = attend_bwd(mg, h, wa[layer], scales, tables, bias, attend_saved)
        attend_grads[layer] = scatter(attend_grad).astype(F32)
        scale_grads[layer] = jnp.concatenate([rows_a, rows_b], axis=0)

    scale_grad = lax.psum(jnp.stack(scale_grads), ("dp", "seq"))
    own_scale = lax.dynamic_slice(scale_grad, (0, s, d * (D // dp)), (LAYERS, 1, D // dp))
    squares = jnp.sum(own_scale * own_scale)
    for part in (*attend_grads, *feed_grads):
        squares = squares + jnp.sum(part * part)
    grad_norm = jnp.sqrt(lax.psum(squares, ("dp", "seq")))

    attend_grad, feed_grad = jnp.stack(attend_grads).astype(BF), jnp.stack(feed_grads).astype(BF)
    triple_grad = moves.tri_back(attend_grad[:, :, :TRI]).astype(F32)
    output_grad = moves.out_back(attend_grad[:, :, TRI:]).astype(F32)
    expand_grad = feed_grad[:, :, :D].astype(F32)
    shrink_grad = moves.shr_back(feed_grad[:, :, D:]).astype(F32)
    return stream, g, grad_norm, (triple_grad, output_grad, expand_grad, shrink_grad, own_scale)


def layers_wide(
    dp, moves, residual, cotangent, scales_weight, tables, bias,
    triple_weight, output_weight, expand_weight, shrink_weight,
):
    d, s, c = lax.axis_index("dp"), lax.axis_index("seq"), moves.c
    sc_own = jnp.zeros((8, 128), F32)
    sc_own = sc_own.at[:LAYERS, : D // dp].set(scales_weight[:, 0].astype(BF).astype(F32))
    pieces = pieces_of(triple_weight, output_weight, expand_weight, shrink_weight, c)
    f = forward_all(dp, residual, sc_own, tables, bias, pieces)
    b = backward_all(dp, cotangent, f, residual, tables, bias)
    half_g, out_g = unpack_rows(b.half_g.astype(F32), c), unpack_rows(b.out_g.astype(F32), c)
    triple_grad = jnp.where(
        c == 0,
        jnp.concatenate([b.whole_g.astype(F32), half_g], axis=-1),
        jnp.concatenate([half_g, b.whole_g.astype(F32)], axis=-1),
    )
    own_scale = lax.dynamic_slice(b.scale_o, (0, s, d * (D // dp)), (LAYERS, 1, D // dp))
    grad_norm = jnp.sqrt(b.norm_o[0, 0])
    return f[0].h_out, b.g_out, grad_norm, (
        triple_grad, out_g, b.exp_g.astype(F32), jnp.swapaxes(b.shr_g, 1, 2).astype(F32), own_scale
    )


def local(dp, *args):
    (residual, cotangent, segments) = args[:3]
    (
        triple_weight, triple_moment, triple_square, triple_shadow,
        output_weight, output_moment, output_square, output_shadow,
        expand_weight, expand_moment, expand_square, expand_shadow,
        shrink_weight, shrink_moment, shrink_square, shrink_shadow,
        scales_weight, scales_moment, scales_square, scales_shadow,
    ) = args[3:]
    moves = Moves(dp)
    t = residual.shape[0]
    d, s = lax.axis_index("dp"), lax.axis_index("seq")
    tables, bias = tables_here(segments, t, moves.x, moves.c)

    if dp == 2 * ZS:
        stream, g, grad_norm, grads = layers_wide(
            dp, moves, residual, cotangent, scales_weight, tables, bias,
            triple_weight, output_weight, expand_weight, shrink_weight,
        )
    else:
        stream, g, grad_norm, grads = layers_narrow(
            dp, moves, residual, cotangent, scales_weight, tables, bias,
            triple_weight, output_weight, expand_weight, shrink_weight,
        )
    triple_grad, output_grad, expand_grad, shrink_grad, own_scale = grads
    limit = CLIP_RATIO * math.sqrt(float(LAYERS * (4 * D * D + 2 * D * FF + 4 * D)))
    factor = limit / (grad_norm + 1e-06)

    results = [stream, g, grad_norm]
    for weight, moment, square, shadow, grad, rate in (
        (triple_weight, triple_moment, triple_square, triple_shadow, triple_grad, RATE_FACTOR / math.sqrt(D)),
        (output_weight, output_moment, output_square, output_shadow, output_grad, RATE_FACTOR / math.sqrt(D // 16)),
        (expand_weight, expand_moment, expand_square, expand_shadow, expand_grad, RATE_FACTOR / math.sqrt(D)),
        (shrink_weight, shrink_moment, shrink_square, shrink_shadow, shrink_grad, RATE_FACTOR / math.sqrt(FF)),
        (scales_weight, scales_moment, scales_square, scales_shadow, own_scale, SCALES_RATE),
    ):
        results.extend(adam_step(weight, moment, square, shadow, grad * factor, rate))
    return tuple(results)


def solution(mesh):
    token = P(("dp", "seq"), None)
    weight = P(None, "dp", "seq")
    scale = P(None, "seq", "dp")
    return jax.shard_map(
        functools.partial(local, mesh.shape["dp"]),
        mesh=mesh,
        in_specs=(token, token, P("dp"), *([weight] * 16), *([scale] * 4)),
        out_specs=(token, token, P(), *([weight] * 16), *([scale] * 4)),
        check_vma=False,
    )
```

profile of v0, /device:TPU:0, one launch (start us, length us, event | category | flops | bytes accessed | tf_op | source)
XLA Modules:
  0.0 347.1 jit_solution(16353000145816150927)
XLA Ops:
  0.7 0.7 convert_bitcast_fusion.1
  1.4 1.3 fusion.25
  4.1 0.6 pad_convert_fusion.refs_1_
  4.7 0.9 convert_element_type.56
  5.7 0.1 fusion.19
  5.8 1.1 convert_element_type.55
  6.9 0.8 slice_select_fusion.refs_4_
  7.7 0.1 fusion.21
  7.8 0.8 maximum_select_fusion.3
  8.6 0.7 convert_element_type.57.refs_7_
  9.3 0.7 convert_bitcast_fusion.refs_8_
  10.1 1.0 multiply_cosine_fusion
  11.1 0.8 pad_maximum_fusion.refs_2_
  11.9 159.9 %forward.1 = (f32[256,768]{1,0:T(8,128)}, f32[256,768]{1,0:T(8,128)}, f32[256,768]{1,0:T(8,128)}, f32[256,768]{1,0:T(8,128)}, f32[2,4,768]{2,1,0:T(4,128)}, /*in...) custom-call(f32[256,768]{1,0:T(8,128)} %refs_18_.1, ...), custom_call_target="tpu_custom_call" | custom-call | flops 23622320128 | bytes 33554432 | tf_op jit(solution)/shard_map/forward/pallas_call | solution.py:1236
  171.8 155.6 %backward.1 = (f32[256,768]{1,0:T(8,128)}, f32[2,4,768]{2,1,0:T(4,128)}, f32[8,128]{1,0:T(8,128)}, bf16[2,96,384]{2,1,0:T(8,128)(2,1)}, bf16[2,144,128]{2,1,0:T(...) custom-call(f32[256,768]{1,0:T(8,128)} %refs_0_.3, ...), custom_call_target="tpu_custom_call" | custom-call | flops 47244640256 | bytes 50331648 | tf_op jit(solution)/shard_map/backward/pallas_call | solution.py:1852
  327.5 1.3 slice.123
  329.6 1.4 multiply_add_fusion.7
  331.0 0.8 slice.146
  331.8 0.9 fusion.24
  332.7 0.1 maximum_select_fusion.1
  332.8 0.8 slice.149
  333.7 0.9 fusion.23
  334.5 0.9 convert_element_type.59
  335.5 2.1 multiply_add_fusion.5
  337.7 1.8 multiply_add_fusion.3
  339.5 1.8 multiply_add_fusion
  341.3 0.1 copy-done.11
  341.4 0.3 copy-done.15
  341.7 1.8 multiply_add_fusion.1
  343.5 0.9 copy.49
  344.4 0.5 copy-done.5
  344.9 0.9 copy.50
  (47 shorter events, 0.2 us)
Async XLA Ops:
  0.7 7.9 %copy-start.1 = (f32[2,96,768]{2,1,0:T(8,128)S(1)}, f32[2,96,768]{2,1,0:T(8,128)}, u32[]{:S(2)}) copy-start(f32[2,96,768]{2,1,0:T(8,128)} %param.36) | copy-start | bytes 1769476
  5.7 3.7 %copy-start = (f32[2,384,192]{1,2,0:T(8,128)S(1)}, f32[2,384,192]{1,2,0:T(8,128)}, u32[]{:S(2)}) copy-start(f32[2,384,192]{1,2,0:T(8,128)} %param.40) | copy-start | bytes 1769476
  171.8 157.8 %copy-start.18 = (f32[2,1,96]{2,1,0:T(1,128)S(1)}, f32[2,1,96]{2,1,0:T(1,128)}, u32[]{:S(2)}) copy-start(f32[2,1,96]{2,1,0:T(1,128)} %param.44) | copy-start | bytes 2308
  171.8 157.8 %copy-start.19 = (f32[2,1,96]{2,1,0:T(1,128)S(1)}, f32[2,1,96]{2,1,0:T(1,128)}, u32[]{:S(2)}) copy-start(f32[2,1,96]{2,1,0:T(1,128)} %param.47) | copy-start | bytes 2308
  171.8 157.8 %copy-start.20 = (f32[2,1,96]{2,1,0:T(1,128)S(1)}, f32[2,1,96]{2,1,0:T(1,128)}, u32[]{:S(2)}) copy-start(f32[2,1,96]{2,1,0:T(1,128)} %param.45) | copy-start | bytes 2308
  171.8 157.8 %copy-start.21 = (f32[2,1,96]{2,1,0:T(1,128)S(1)}, f32[2,1,96]{2,1,0:T(1,128)}, u32[]{:S(2)}) copy-start(f32[2,1,96]{2,1,0:T(1,128)} %param.46) | copy-start | bytes 2308
  171.8 163.7 %copy-start.17 = (f32[2,96,192]{2,1,0:T(8,128)S(1)}, f32[2,96,192]{2,1,0:T(8,128)}, u32[]{:S(2)}) copy-start(f32[2,96,192]{2,1,0:T(8,128)} %param.35) | copy-start | bytes 442372
  327.5 8.0 %copy-start.3 = (f32[2,96,192]{2,1,0:T(8,128)S(1)}, f32[2,96,192]{2,1,0:T(8,128)}, u32[]{:S(2)}) copy-start(f32[2,96,192]{2,1,0:T(8,128)} %param.32) | copy-start | bytes 442372
  327.5 10.2 %copy-start.2 = (f32[2,96,576]{2,1,0:T(8,128)S(1)}, f32[2,96,576]{2,1,0:T(8,128)}, u32[]{:S(2)}) copy-start(f32[2,96,576]{2,1,0:T(8,128)} %param.28) | copy-start | bytes 1327108
  327.5 10.2 %copy-start.12 = (f32[2,96,576]{2,1,0:T(8,128)S(1)}, f32[2,96,576]{2,1,0:T(8,128)}, u32[]{:S(2)}) copy-start(f32[2,96,576]{2,1,0:T(8,128)} %param.31) | copy-start | bytes 1327108
  327.5 10.1 %copy-start.13 = (f32[2,96,576]{2,1,0:T(8,128)S(1)}, f32[2,96,576]{2,1,0:T(8,128)}, u32[]{:S(2)}) copy-start(f32[2,96,576]{2,1,0:T(8,128)} %param.29) | copy-start | bytes 1327108
  327.5 10.1 %copy-start.14 = (f32[2,96,576]{2,1,0:T(8,128)S(1)}, f32[2,96,576]{2,1,0:T(8,128)}, u32[]{:S(2)}) copy-start(f32[2,96,576]{2,1,0:T(8,128)} %param.30) | copy-start | bytes 1327108
  337.7 1.8 copy-start.6
  337.7 1.8 copy-start.7
  337.7 1.8 copy-start.8
  337.7 1.8 copy-start.16
  339.5 1.8 copy-start.9
  339.5 1.8 copy-start.10
  339.5 1.9 copy-start.11
  339.5 2.2 copy-start.15
  341.7 1.8 copy-start.4
  343.5 1.4 copy-start.5
where the time goes:
time: 353 us; the launch traced here: 347 us
  Pallas kernels  315 us (89%)
  other arithmetic  18.2 us (5%)
  local copies, waits for them, and re-layouts  9.09 us (3%)
  between operations  4.36 us (1%)
    pallas_call x1, Pallas kernels, forward_all(): pl.pallas_call(functools.partial(fwd_kernel, dp), name='forward', out_sha...  160 us
    pallas_call x1, Pallas kernels, backward_all(): pl.pallas_call(functools.partial(bwd_kernel, dp), name='backward', out_sh...  156 us
    add x5, other arithmetic, adam_step(): average = shadow_decay * shadow + (1.0 - shadow_decay) * updated  8.84 us

commit v1 on v0

--- a/solution.py
+++ b/solution.py
@@ -655,6 +655,7 @@
     na: Any
     q: Any
     k: Any
+    k_t: Any
     v: Any
     ctx: Any
     ctx_t: Any
@@ -670,14 +671,14 @@
 
 class ForwardIn(NamedTuple):
     h0: Any
-    sc_own: Any
+    g0: Any
+    sc_w: Any
     cs: Any
     bias: Any
-    p_whole: Any
-    p_half: Any
-    p_out: Any
-    p_exp: Any
-    p_shr: Any
+    tri_w: Any
+    out_w: Any
+    exp_w: Any
+    shr_w: Any
 
 
 class ForwardHead(NamedTuple):
@@ -686,9 +687,16 @@
     mid_o0: Any
     mid_o1: Any
     sc_o: Any
+    gl_o: Any
 
 
 class ForwardScratch(NamedTuple):
+    p_whole: Any
+    p_half: Any
+    p_out: Any
+    p_exp: Any
+    p_shr: Any
+    gl: Any
     wt: Any
     wo: Any
     we: Any
@@ -708,6 +716,8 @@
     nb: Any
     na_t: Any
     nb_t: Any
+    k_t: Any
+    v_t: Any
     act: Any
     slope: Any
     psend: Any
@@ -929,7 +939,10 @@
 def gather_scales_start(w):
     n = w.n
     mine = n.scl.at[w.y, w.z, w.s]
-    mine[...] = n.sc_own[...]
+    mine[...] = jnp.zeros_like(mine)
+    wide = n.sc_w.shape[-1]
+    for layer in range(LAYERS):
+        mine[layer : layer + 1, 0:wide] = n.sc_w[layer].astype(BF).astype(F32)
 
     def one(i, carry):
         z, s = lax.div(i, SEQ), lax.rem(i, SEQ)
@@ -985,24 +998,56 @@
     ins, outs, saved0, saved1, scratch = split(refs, ForwardIn, ForwardHead, Saved, Saved, ForwardScratch)
     n = Refs(ins, outs, scratch)
     saved = (saved0, saved1)
-    rows = n.p_exp.shape[1]
+    rows = n.exp_w.shape[1]
     t = n.h0.shape[0]
     w = Weights(n, rows)
     x, c, peer, sib = w.x, w.c, w.peer, w.sib
     y = 1 - x
+    parts = (pl.ds(0, t // 2), pl.ds(t // 2, t // 2))
     copies = Copies(n.lsem, n.xs, n.xr, w.d)
     waits = []
 
     def save(src, dst):
         waits.append(copies.local(src, dst))
 
+    half_rows = rows // 2
+
+    def pack(low, into, layer, core):
+        wide, rest = (low[:, :128], low[:, 128:]) if core == 0 else (low[:, 64:], low[:, :64])
+        ends = [rest[:half_rows], rest[half_rows:]]
+        into[layer, pl.ds(0, rows), :] = wide.astype(BF)
+        into[layer, pl.ds(rows, half_rows), :] = jnp.concatenate(ends if core == 0 else ends[::-1], axis=1).astype(BF)
+
+    def round_triple(layer):
+        for core in range(2):
+
+            @pl.when(c == core)
+            def _():
+                tri = n.tri_w[layer]
+                n.p_whole[layer] = (tri[:, :HALF] if core == 0 else tri[:, 192:]).astype(BF)
+                pack(tri[:, HALF:] if core == 0 else tri[:, :192], n.p_half, layer, core)
+
+    def round_output(layer):
+        for core in range(2):
+            pl.when(c == core)(lambda: pack(n.out_w[layer], n.p_out, layer, core))
+
+    round_triple(0)
     greet_all(w)
     w.zero(TRIPLE, 0)
     gather_scales_start(w)
-    for kind in (OUTPUT, EXPAND, SHRINK):
-        w.zero(kind, 0)
-    w.spread(TRIPLE, 0)
-    w.spread(OUTPUT, 0)
+    round_output(0)
+    w.zero(OUTPUT, 0)
+    n.p_exp[...] = n.exp_w[...].astype(BF)
+    w.zero(EXPAND, 0)
+    n.p_shr[...] = n.shr_w[...].astype(BF)
+    w.zero(SHRINK, 0)
+    round_triple(1)
+    round_output(1)
+    for kind in KINDS:
+        w.zero(kind, 1)
+    for layer in range(LAYERS):
+        for kind in KINDS:
+            w.spread(kind, layer)
     n.hs[0] = n.h0[...]
     xhat, _ = norm_stats(n.hs[0])
     gather_scales_end(w)
@@ -1029,13 +1074,12 @@
             xhat, _ = norm_stats(n.hs[layer])
         n.na[layer, x] = (xhat * n.sc[layer, 0:1, :] + n.sc[layer, 1:2, :]).astype(BF)
         na_sent = copies.push(n.na.at[layer, x], n.na.at[layer, x], peer)
+        if last:
+            n.gl[x] = n.g0[...].astype(BF)
+            gl_sent = copies.push(n.gl.at[x], n.gl.at[x], peer)
         if layer == 0:
             w.onward_all(TRIPLE, 0)
-            w.spread(EXPAND, 0)
-            w.spread(SHRINK, 0)
             w.onward_all(OUTPUT, 0)
-            for kind in KINDS:
-                w.zero(kind, 1)
             w.arrive(TRIPLE, 0)
             tri_sent = share_tri(0)
         tri_sent.wait()
@@ -1068,6 +1112,8 @@
         out_sent = share_out(layer)
         for copy in shared:
             copy.wait()
+        for block in range(2):
+            n.v_t[block] = n.v[layer, block].T
         save(n.q.at[layer], saved[layer].q)
         save(n.k.at[layer], saved[layer].k)
         save(n.v.at[layer], saved[layer].v)
@@ -1080,7 +1126,6 @@
                 lanes = pl.ds(pl.multiple_of(p * 128, 128), 128)
                 q_pair = n.q[layer, block, :, lanes]
                 k_same, k_cross = n.k[layer, block, :, lanes], n.k[layer, other, :, lanes]
-                v_same, v_cross = n.v[layer, block, :, lanes], n.v[layer, other, :, lanes]
                 for which in range(2):
                     q_head = half_of(q_pair, which)
                     s_same = nt(k_same, q_head)
@@ -1093,9 +1138,9 @@
                     total = jnp.sum(e_same, axis=0, keepdims=True) + jnp.sum(
                         e_cross, axis=0, keepdims=True
                     )
-                    mixed = tn(v_same, e_same.astype(BF)) + tn(v_cross, e_cross.astype(BF))
                     head = pl.ds(pl.multiple_of(p * 128 + which * HD, HD), HD)
-                    n.ctxt[head, :] = mixed[which * HD : which * HD + HD, :] / total
+                    mixed = nn(n.v_t[block, head, :], e_same.astype(BF)) + nn(n.v_t[other, head, :], e_cross.astype(BF))
+                    n.ctxt[head, :] = mixed / total
                     n.lse[layer, block, pl.ds(2 * p + which, 1), :] = top + jnp.log(total)
                 return carry
 
@@ -1108,14 +1153,14 @@
             pl.when(p > 0)(lambda: w.onward(kind, layer, p - 1))
 
         attend(y, early)
+        if last:
+            gl_sent.wait()
+            save(n.gl, n.gl_o)
         out_sent.wait()
         use = 2 * layer
         n.psend[use] = nn(n.ctx[layer, y], n.wo[layer]).astype(BF)
         part_sent = copies.push(n.psend.at[use], n.precv.at[use], peer)
 
-        if not last:
-            w.spread(TRIPLE, layer + 1)
-            w.spread(OUTPUT, layer + 1)
 
         def late(p):
             if layer == 0:
@@ -1124,9 +1169,6 @@
                 pl.when(p > 0)(lambda: w.onward(SHRINK, layer, p - 1))
 
         attend(x, late)
-        if not last:
-            w.spread(EXPAND, layer + 1)
-            w.spread(SHRINK, layer + 1)
         n.mid[layer] = n.hs[layer] + nn(n.ctx[layer, x], n.wo[layer])
         save(n.ctx.at[layer], saved[layer].ctx)
         save(n.lse.at[layer], saved[layer].lse)
@@ -1135,27 +1177,30 @@
         save(n.ctx_t.at[layer], saved[layer].ctx_t)
         for block in range(2):
             n.na_t[layer, :, block * t : block * t + t] = n.na[layer, block].T
+            n.k_t[layer, block] = n.k[layer, block].T
         save(n.na_t.at[layer], saved[layer].na)
+        save(n.k_t.at[layer], saved[layer].k_t)
         part_sent.wait()
         n.mid[layer] = n.mid[layer] + n.precv[use].astype(F32)
         save(n.mid.at[layer], (n.mid_o0, n.mid_o1)[layer])
 
         xhat, _ = norm_stats(n.mid[layer])
         n.nb[layer, x] = (xhat * n.sc[layer, 2:3, :] + n.sc[layer, 3:4, :]).astype(BF)
-        nb_sent = copies.push(n.nb.at[layer, x], n.nb.at[layer, x], peer)
+        nb_sent = [copies.push(n.nb.at[layer, x, part], n.nb.at[layer, x, part], peer) for part in parts]
         w.arrive(EXPAND, layer)
         exp_sent = share_exp(layer)
         w.arrive(SHRINK, layer)
         shr_sent = share_shr(layer)
         exp_sent.wait()
-
-        def feed(block, pump):
+        save(n.we.at[layer], saved[layer].we)
+
+        def feed(block, part, pump):
             def step(i, carry):
                 pump(i)
                 lanes = pl.ds(pl.multiple_of(i * 256, 256), 256)
-                value, rate = gelu_parts(nn(n.nb[layer, block], n.we[layer, :, lanes]))
-                n.act[layer, block, :, lanes] = value.astype(BF)
-                n.slope[layer, block, :, lanes] = rate.astype(BF)
+                value, rate = gelu_parts(nn(n.nb[layer, block, part, :], n.we[layer, :, lanes]))
+                n.act[layer, block, part, lanes] = value.astype(BF)
+                n.slope[layer, block, part, lanes] = rate.astype(BF)
                 return carry
 
             lax.fori_loop(0, HID // 256, step, 0)
@@ -1168,26 +1213,28 @@
                     w.onward(TRIPLE, layer + 1, i)
                     w.onward(OUTPUT, layer + 1, i)
 
-        feed(x, lambda i: None)
+        feed(x, pl.ds(0, t), lambda i: None)
         shr_sent.wait()
+        save(n.ws.at[layer], saved[layer].ws)
         n.hs[layer + 1] = n.mid[layer] + nt(n.act[layer, x], n.ws[layer])
-        nb_sent.wait()
-        feed(y, pump)
         use = 2 * layer + 1
-        n.psend[use] = nt(n.act[layer, y], n.ws[layer]).astype(BF)
-        part_sent = copies.push(n.psend.at[use], n.precv.at[use], peer)
+        part_sent = []
+        for number, part in enumerate(parts):
+            nb_sent[number].wait()
+            feed(y, part, pump if number == 0 else lambda i: None)
+            n.psend[use, part, :] = nt(n.act[layer, y, part, :], n.ws[layer]).astype(BF)
+            part_sent.append(copies.push(n.psend.at[use, part], n.precv.at[use, part], peer))
         for block in range(2):
             n.nb_t[layer, :, block * t : block * t + t] = n.nb[layer, block].T
         save(n.nb_t.at[layer], saved[layer].nb)
         save(n.act.at[layer], saved[layer].act)
         save(n.slope.at[layer], saved[layer].slope)
-        save(n.we.at[layer], saved[layer].we)
-        save(n.ws.at[layer], saved[layer].ws)
         if not last:
             w.onward_all(EXPAND, layer + 1)
             w.arrive(TRIPLE, layer + 1)
             tri_sent = share_tri(layer + 1)
-        part_sent.wait()
+        for copy in part_sent:
+            copy.wait()
         n.hs[layer + 1] = n.hs[layer + 1] + n.precv[use].astype(F32)
 
     n.h_out[...] = n.hs[LAYERS]
@@ -1200,19 +1247,23 @@
             w.finish(kind, layer)
 
 
-def forward_all(dp, h, sc_own, tables, bias, pieces):
+def forward_all(dp, h, g, scales_weight, tables, bias, shards):
     t = h.shape[0]
     zs, packed = dp // 2, 3 * (D // dp) // 2
     per_layer = [
-        sds((D, 2 * t), BF), sds((2, t, HALF), BF), sds((2, 2 * t, HALF), BF), sds((2, 2 * t, HALF), BF),
+        sds((D, 2 * t), BF), sds((2, t, HALF), BF), sds((2, 2 * t, HALF), BF), sds((2, HALF, 2 * t), BF), sds((2, 2 * t, HALF), BF),
         sds((2, t, HALF), BF), sds((HALF, 2 * t), BF), sds((2, 8, t), F32), sds((D, 2 * t), BF), sds((2, t, HID), BF),
         sds((2, t, HID), BF), sds((D, TRI), BF), sds((HALF, D), BF), sds((D, HID), BF), sds((D, HID), BF),
     ]
     token = sds((t, D), F32)
-    outs = [token, token, token, token, sds((LAYERS, 4, D), F32), *per_layer, *per_layer]
-    specs = [vmem(), hbm(), hbm(), hbm(), vmem(), *([hbm()] * (2 * len(per_layer)))]
+    outs = [token, token, token, token, sds((LAYERS, 4, D), F32), sds((2, t, D), BF), *per_layer, *per_layer]
+    specs = [vmem(), hbm(), hbm(), hbm(), vmem(), hbm(), *([hbm()] * (2 * len(per_layer)))]
     n_layers = LAYERS
+    rows = D // dp
     scratch = [
+        pltpu.VMEM((n_layers, rows, HALF), BF), pltpu.VMEM((n_layers, packed, 128), BF),
+        pltpu.VMEM((n_layers, packed, 128), BF), pltpu.VMEM((n_layers, rows, D), BF),
+        pltpu.VMEM((n_layers, 192, 4 * rows), BF), pltpu.VMEM((2, t, D), BF),
         pltpu.VMEM((n_layers, D, TRI), BF), pltpu.VMEM((n_layers, HALF, D), BF),
         pltpu.VMEM((n_layers, D, HID), BF), pltpu.VMEM((n_layers, D, HID), BF),
         pltpu.VMEM((n_layers, 2, packed, 128), BF), pltpu.VMEM((n_layers, 2, packed, 128), BF),
@@ -1223,6 +1274,7 @@
         pltpu.VMEM((n_layers, 2, t, HALF), BF), pltpu.VMEM((n_layers, HALF, 2 * t), BF),
         pltpu.VMEM((n_layers, 2, 8, t), F32), pltpu.VMEM((n_layers, 2, t, D), BF),
         pltpu.VMEM((n_layers, D, 2 * t), BF), pltpu.VMEM((n_layers, D, 2 * t), BF),
+        pltpu.VMEM((n_layers, 2, HALF, 2 * t), BF), pltpu.VMEM((2, HALF, 2 * t), BF),
         pltpu.VMEM((n_layers, 2, t, HID), BF),
         pltpu.VMEM((n_layers, 2, t, HID), BF), pltpu.VMEM((2 * n_layers, t, D), BF),
         pltpu.VMEM((2 * n_layers, t, D), BF), pltpu.VMEM((n_layers + 1, t, D), F32),
@@ -1231,44 +1283,21 @@
         pltpu.SemaphoreType.DMA((n_layers, len(KINDS), 2, zs)),
         pltpu.SemaphoreType.DMA((n_layers, len(KINDS), 2)), pltpu.SemaphoreType.DMA((n_layers, len(KINDS), 4)),
         pltpu.SemaphoreType.DMA((zs * SEQ + 1,)), pltpu.SemaphoreType.DMA((zs * SEQ + 1,)),
-        pltpu.SemaphoreType.DMA((24,)), pltpu.SemaphoreType.DMA((24,)), pltpu.SemaphoreType.DMA((32,)),
+        pltpu.SemaphoreType.DMA((32,)), pltpu.SemaphoreType.DMA((32,)), pltpu.SemaphoreType.DMA((40,)),
     ]
     results = pl.pallas_call(
         functools.partial(fwd_kernel, dp),
         name="forward",
         out_shape=outs,
-        in_specs=[vmem(), vmem(), vmem(), pl.BlockSpec(memory_space=pltpu.SMEM), *([hbm()] * 5)],
+        in_specs=[*([vmem()] * 4), pl.BlockSpec(memory_space=pltpu.SMEM), *([vmem()] * 4)],
         out_specs=specs,
         scratch_shapes=scratch,
         cost_estimate=pl.CostEstimate(flops=22 << 30, bytes_accessed=32 << 20, transcendentals=0),
         compiler_params=pltpu.CompilerParams(
             collective_id=4, has_side_effects=True, vmem_limit_bytes=VMEM_BYTES
         ),
-    )(h, sc_own, tables, bias, *pieces)
+    )(h, g, scales_weight, tables, bias, *shards)
     return split(results, ForwardHead, Saved, Saved)
-
-
-def pack_rows(low, c):
-    half = low.shape[1] // 2
-    even = [low[:, :, :128], jnp.concatenate([low[:, :half, 128:], low[:, half:, 128:]], axis=2)]
-    odd = [low[:, :, 64:], jnp.concatenate([low[:, half:, :64], low[:, :half, :64]], axis=2)]
-    return jnp.where(c == 0, jnp.concatenate(even, axis=1), jnp.concatenate(odd, axis=1))
-
-
-def unpack_rows(packed, c):
-    rows = 2 * packed.shape[1] // 3
-    wide, rest = packed[:, :rows], packed[:, rows:]
-    even = jnp.concatenate([wide, jnp.concatenate([rest[:, :, :64], rest[:, :, 64:]], axis=1)], axis=2)
-    odd = jnp.concatenate([jnp.concatenate([rest[:, :, 64:], rest[:, :, :64]], axis=1), wide], axis=2)
-    return jnp.where(c == 0, even, odd)
-
-
-def pieces_of(triple_weight, output_weight, expand_weight, shrink_weight, c):
-    tri = triple_weight.astype(BF)
-    whole = jnp.where(c == 0, tri[:, :, :HALF], tri[:, :, 192:])
-    half = jnp.where(c == 0, tri[:, :, HALF:], tri[:, :, :192])
-    shr = jnp.swapaxes(shrink_weight.astype(BF), 1, 2)
-    return whole, pack_rows(half, c), pack_rows(output_weight.astype(BF), c), expand_weight.astype(BF), shr
 
 
 class Sums(Spot):
@@ -1463,6 +1492,7 @@
     na: Any
     q: Any
     k: Any
+    k_t: Any
     v: Any
     ctx: Any
     ctx_t: Any
@@ -1480,6 +1510,7 @@
 
 class BackwardIn(NamedTuple):
     g0: Any
+    gl_h: Any
     sc: Any
     cs: Any
     bias: Any
@@ -1489,8 +1520,7 @@
     g_out: Any
     scale_o: Any
     norm_o: Any
-    whole_g: Any
-    half_g: Any
+    tri_g: Any
     out_g: Any
     exp_g: Any
     shr_g: Any
@@ -1564,6 +1594,7 @@
     w = Sums(n, D // dp)
     x, c, peer, sib = w.x, w.c, w.peer, w.sib
     y = 1 - x
+    parts = (pl.ds(0, t // 2), pl.ds(t // 2, t // 2))
     copies = Copies(n.lsem, n.xs, n.xr, w.d)
     loading = {}
 
@@ -1575,9 +1606,10 @@
         for place in wanted:
             loading[place].wait()
 
-    na, q, k, v, ctx, ctx_t, lse, nb, act, slope, wt, wo, we, ws, h, mid = range(len(Loaded._fields))
+    na, q, k, k_t, v, ctx, ctx_t, lse, nb, act, slope, wt, wo, we, ws, h, mid = range(len(Loaded._fields))
     feed_places = (ws, slope, we, act, nb, mid)
-    attend_places = (wo, ctx, q, k, v, lse, wt, na, ctx_t, h)
+    attend_places = (wo, ctx, q, k, v, lse, k_t, wt, na, ctx_t, h)
+    top_gl = copies.local(n.gl_h, n.gl.at[LAYERS - 1])
     load(LAYERS - 1, *feed_places, *attend_places)
     greet_all(w)
     n.g_out[...] = n.g0[...]
@@ -1585,20 +1617,22 @@
     for layer in reversed(range(LAYERS)):
         top = layer == LAYERS - 1
 
-        n.gl[layer, x] = n.g_out[...].astype(BF)
-        g_sent = copies.push(n.gl.at[layer, x], n.gl.at[layer, x], peer)
+        if top:
+            top_gl.wait()
+        else:
+            n.gl[layer, x] = n.g_out[...].astype(BF)
+            g_sent = [copies.push(n.gl.at[layer, x, part], n.gl.at[layer, x, part], peer) for part in parts]
         ready(ws, slope, we)
 
-        def back(block, pump):
+        def back(block, part):
             def step(i, carry):
-                pump(i)
                 lanes = pl.ds(pl.multiple_of(i * 256, 256), 256)
-                pulled = nn(n.gl[layer, block], n.ws[:, lanes])
-                n.hg[block, :, lanes] = (pulled * n.slope[block, :, lanes].astype(F32)).astype(BF)
+                pulled = nn(n.gl[layer, block, part, :], n.ws[:, lanes])
+                n.hg[block, part, lanes] = (pulled * n.slope[block, part, lanes].astype(F32)).astype(BF)
                 return carry
 
             lax.fori_loop(0, HID // 256, step, 0)
-            return nt(n.hg[block], n.we[...])
+            return nt(n.hg[block, part, :], n.we[...])
 
         def pump_tri(i):
             if not top:
@@ -1608,11 +1642,14 @@
                     w.along(TRIPLE, layer + 1, i)
                     w.along(OUTPUT, layer + 1, i)
 
-        n.part[...] = back(x, lambda i: None)
-        g_sent.wait()
+        n.part[...] = back(x, pl.ds(0, t))
         use = 2 * layer
-        n.psend[...] = back(y, lambda i: None).astype(BF)
-        part_sent = copies.push(n.psend, n.precv.at[use], peer)
+        part_sent = []
+        for number, part in enumerate(parts):
+            if not top:
+                g_sent[number].wait()
+            n.psend[part, :] = back(y, part).astype(BF)
+            part_sent.append(copies.push(n.psend.at[part], n.precv.at[use, part], peer))
         ready(act, nb, mid)
         for block in range(2):
             n.gl_t[:, block * t : block * t + t] = n.gl[layer, block].T
@@ -1657,7 +1694,8 @@
         shr_sent.wait()
         lax.fori_loop(0, HID // 256, keep_shr, 0)
         w.across_all(SHRINK, layer)
-        part_sent.wait()
+        for copy in part_sent:
+            copy.wait()
         dy = n.part[...] + n.precv[use].astype(F32)
         back_mid, rows_b = norm_back(n.mid[...], n.sc[layer, 2:3, :], dy)
         n.g_out[...] = n.g_out[...] + back_mid
@@ -1668,7 +1706,7 @@
             load(layer - 1, *feed_places)
         n.dk[...] = jnp.zeros_like(n.dk)
         n.dv[...] = jnp.zeros_like(n.dv)
-        ready(wo, ctx, q, k, v, lse)
+        ready(wo, ctx, q, k, v, lse, k_t)
 
         def attend(block, pump):
             other = 1 - block
@@ -1688,6 +1726,7 @@
                     row = pl.ds(2 * p + which, 1)
                     total, dots = n.lse[block, row, :], n.delta[row, :]
                     turned = None
+                    head = pl.ds(pl.multiple_of(p * 128 + which * HD, HD), HD)
                     for side in (block, other):
                         k_pair, v_pair = n.k[side, :, lanes], n.v[side, :, lanes]
                         scores = nt(k_pair, q_head)
@@ -1697,10 +1736,9 @@
                         score_grad = (probs * (nt(v_pair, cg_head) - dots)).astype(BF)
                         n.dv[side, :, lanes] += nn(probs.astype(BF), cg_head)
                         n.dk[side, :, lanes] += nn(score_grad, q_head)
-                        piece = tn(k_pair, score_grad)
+                        piece = nn(n.k_t[side, head, :], score_grad)
                         turned = piece if turned is None else turned + piece
-                    head = pl.ds(pl.multiple_of(p * 128 + which * HD, HD), HD)
-                    n.dqt[block, head, :] = turned[which * HD : which * HD + HD, :] * HD**-0.5
+                    n.dqt[block, head, :] = turned * HD**-0.5
                 return carry
 
             lax.fori_loop(0, HALF // 128, pair_step, 0)
@@ -1801,11 +1839,31 @@
     for layer in range(LAYERS):
         for kind in KINDS:
             w.home(kind, layer)
+    rows = D // dp
+
+    def natural(packed):
+        wide, rest = packed[:rows].astype(F32), packed[rows:].astype(F32)
+        even = jnp.concatenate([rest[:, :HD], rest[:, HD:]], axis=0)
+        odd = jnp.concatenate([rest[:, HD:], rest[:, :HD]], axis=0)
+        return jnp.concatenate([wide, even], axis=1), jnp.concatenate([odd, wide], axis=1)
+
+    for layer in range(LAYERS):
+        halves, outs_here = natural(n.f_half[layer]), natural(n.f_out[layer])
+        whole = n.f_whole[layer].astype(F32)
+
+        @pl.when(c == 0)
+        def _():
+            n.tri_g[layer] = jnp.concatenate([whole, halves[0]], axis=1)
+            n.out_g[layer] = outs_here[0]
+
+        @pl.when(c == 1)
+        def _():
+            n.tri_g[layer] = jnp.concatenate([halves[1], whole], axis=1)
+            n.out_g[layer] = outs_here[1]
+
     outputs = [
         copies.local(a, b)
-        for a, b in (
-            (n.f_whole, n.whole_g), (n.f_half, n.half_g), (n.f_out, n.out_g), (n.f_exp, n.exp_g), (n.f_shr, n.shr_g)
-        )
+        for a, b in ((n.f_exp, n.exp_g), (n.f_shr, n.shr_g))
     ]
     total = everywhere_end(w, 2, n.sq, n.sq_pair)
     n.norm_o[...] = total + squared(first[0:6]) + squared(second)
@@ -1824,8 +1882,8 @@
     head, saved0, saved1 = f
     saved = (*saved0, residual, head.mid_o0, *saved1, head.h_mid, head.mid_o1)
     outs = [
-        sds((t, D), F32), sds((LAYERS, 4, D), F32), sds((8, 128), F32), sds((LAYERS, r, HALF), BF),
-        sds((LAYERS, packed, 128), BF), sds((LAYERS, packed, 128), BF), sds((LAYERS, r, D), BF),
+        sds((t, D), F32), sds((LAYERS, 4, D), F32), sds((8, 128), F32), sds((LAYERS, r, TRI // 2), F32),
+        sds((LAYERS, r, 192), F32), sds((LAYERS, r, D), BF),
         sds((LAYERS, 192, 4 * r), BF),
     ]
     v = pltpu.VMEM
@@ -1847,20 +1905,20 @@
         pltpu.SemaphoreType.DMA((ll, len(KINDS), 2, zs)), pltpu.SemaphoreType.DMA((ll, len(KINDS), 2, zs)),
         pltpu.SemaphoreType.DMA((ll, len(KINDS), 4)), pltpu.SemaphoreType.DMA((ll, len(KINDS), 2)),
         pltpu.SemaphoreType.DMA((3, zs * SEQ + 1)), pltpu.SemaphoreType.DMA((3, zs * SEQ + 1)),
-        pltpu.SemaphoreType.DMA((20,)), pltpu.SemaphoreType.DMA((20,)), pltpu.SemaphoreType.DMA((40,)),
+        pltpu.SemaphoreType.DMA((28,)), pltpu.SemaphoreType.DMA((28,)), pltpu.SemaphoreType.DMA((48,)),
     ]
     results = pl.pallas_call(
         functools.partial(bwd_kernel, dp),
         name="backward",
         out_shape=outs,
-        in_specs=[vmem(), vmem(), vmem(), pl.BlockSpec(memory_space=pltpu.SMEM), *([hbm()] * len(saved))],
-        out_specs=[vmem()] * 3 + [hbm()] * 5,
+        in_specs=[vmem(), hbm(), vmem(), vmem(), pl.BlockSpec(memory_space=pltpu.SMEM), *([hbm()] * len(saved))],
+        out_specs=[vmem()] * 5 + [hbm()] * 2,
         scratch_shapes=scratch,
         cost_estimate=pl.CostEstimate(flops=44 << 30, bytes_accessed=48 << 20, transcendentals=0),
         compiler_params=pltpu.CompilerParams(
             collective_id=5, has_side_effects=True, vmem_limit_bytes=VMEM_BYTES
         ),
-    )(g, head.sc_o, tables, bias, *saved)
+    )(g, head.gl_o, head.sc_o, tables, bias, *saved)
     return BackwardOut(*results)
 
 
@@ -2053,22 +2111,14 @@
     dp, moves, residual, cotangent, scales_weight, tables, bias,
     triple_weight, output_weight, expand_weight, shrink_weight,
 ):
-    d, s, c = lax.axis_index("dp"), lax.axis_index("seq"), moves.c
-    sc_own = jnp.zeros((8, 128), F32)
-    sc_own = sc_own.at[:LAYERS, : D // dp].set(scales_weight[:, 0].astype(BF).astype(F32))
-    pieces = pieces_of(triple_weight, output_weight, expand_weight, shrink_weight, c)
-    f = forward_all(dp, residual, sc_own, tables, bias, pieces)
+    d, s = lax.axis_index("dp"), lax.axis_index("seq")
+    shards = (triple_weight, output_weight, expand_weight, jnp.swapaxes(shrink_weight, 1, 2))
+    f = forward_all(dp, residual, cotangent, scales_weight, tables, bias, shards)
     b = backward_all(dp, cotangent, f, residual, tables, bias)
-    half_g, out_g = unpack_rows(b.half_g.astype(F32), c), unpack_rows(b.out_g.astype(F32), c)
-    triple_grad = jnp.where(
-        c == 0,
-        jnp.concatenate([b.whole_g.astype(F32), half_g], axis=-1),
-        jnp.concatenate([half_g, b.whole_g.astype(F32)], axis=-1),
-    )
     own_scale = lax.dynamic_slice(b.scale_o, (0, s, d * (D // dp)), (LAYERS, 1, D // dp))
     grad_norm = jnp.sqrt(b.norm_o[0, 0])
     return f[0].h_out, b.g_out, grad_norm, (
-        triple_grad, out_g, b.exp_g.astype(F32), jnp.swapaxes(b.shr_g, 1, 2).astype(F32), own_scale
+        b.tri_g, b.out_g, b.exp_g.astype(F32), jnp.swapaxes(b.shr_g, 1, 2).astype(F32), own_scale
     )
 
 

time: 353 us -> 330 us (0.935)
  Pallas kernels: 315 us -> 305 us
  other arithmetic: 18.2 us -> 11.4 us
    pallas_call x1, Pallas kernels: 156 us -> 150 us  [backward_all(): pl.pallas_call(functools.partial(bwd_kernel, dp), name='backward', out_sh...]
    convert_element_type x5 -> x0, other arithmetic: 4.47 us -> none  [the longest x1 1.12 us: pieces_of(): tri = triple_weight.astype(BF)]
    pallas_call x1, Pallas kernels: 160 us -> 155 us  [forward_all(): pl.pallas_call(functools.partial(fwd_kernel, dp), name='forward', out_sha...]
    slice x8 -> x0, local copies, waits for them, and re-layouts: 3.61 us -> none  [the longest x2 1.62 us: unpack_rows(): wide, rest = (packed[:, :rows], packed[:, rows:])]
where the time goes in v1:
time: 330 us; the launch traced here: 327 us
  Pallas kernels  305 us (92%)
  other arithmetic  11.4 us (3%)
  local copies, waits for them, and re-layouts  5.77 us (2%)
  between operations  4.33 us (1%)
    pallas_call x1, Pallas kernels, forward_all(): pl.pallas_call(functools.partial(fwd_kernel, dp), name='forward', out_sha...  155 us
    pallas_call x1, Pallas kernels, backward_all(): pl.pallas_call(functools.partial(bwd_kernel, dp), name='backward', out_sh...  150 us
    add x5, other arithmetic, adam_step(): average = shadow_decay * shadow + (1.0 - shadow_decay) * updated  9.55 us

profile of v1, /device:TPU:0, one launch (start us, length us, event | category | flops | bytes accessed | tf_op | source)
XLA Modules:
  0.0 326.8 jit_solution(9937379385083004242)
XLA Ops:
  0.7 1.3 fusion.17
  3.4 1.0 multiply_cosine_fusion
  4.4 0.8 pad_maximum_fusion.refs_3_
  5.2 155.4 %forward.1 = (f32[256,768]{1,0:T(8,128)}, f32[256,768]{1,0:T(8,128)}, f32[256,768]{1,0:T(8,128)}, f32[256,768]{1,0:T(8,128)}, f32[2,4,768]{2,1,0:T(4,128)}, /*in...) custom-call(f32[256,768]{1,0:T(8,128)} %refs_20_.1, ...), custom_call_target="tpu_custom_call" | custom-call | flops 23622320128 | bytes 33554432 | tf_op jit(solution)/shard_map/forward/pallas_call | solution.py:1288
  160.6 0.0 copy-start.20
  160.6 0.0 copy-start.21
  160.6 0.0 copy-start.22
  160.6 0.0 copy-start.23
  160.7 0.0 copy-start.16
  160.7 0.0 copy-start.17
  160.7 0.0 copy-start.18
  160.7 0.0 copy-start.19
  160.7 149.9 %backward.1 = (f32[256,768]{1,0:T(8,128)}, f32[2,4,768]{2,1,0:T(4,128)}, f32[8,128]{1,0:T(8,128)}, f32[2,96,576]{2,1,0:T(8,128)}, f32[2,96,192]{2,1,0:T(8,128)},...) custom-call(f32[256,768]{1,0:T(8,128)} %refs_0_.3, bf16[2,256,768]{2,1,0:T(8,128)(2,1)} %get-tuple-element.67.refs_1_, ...), custom_call_target="tpu_custom_call" | custom-call | flops 47244640256 | bytes 50331648 | tf_op jit(solution)/shard_map/backward/pallas_call | solution.py:1910
  310.7 0.0 copy-start.10
  310.7 0.0 copy-start.11
  310.7 1.3 slice.11
  312.8 1.4 multiply_add_fusion.7
  314.2 1.9 multiply_add_fusion.5
  316.1 0.0 copy-start.3
  316.1 0.0 copy-start.4
  316.2 2.7 multiply_add_fusion.3
  318.9 0.0 copy-start.6
  318.9 0.0 copy-start.8
  319.0 0.0 copy-start.9
  319.0 1.8 multiply_add_fusion
  320.8 0.1 copy-done.8
  320.8 0.6 copy-done.9
  321.4 0.1 copy-done.14
  321.5 1.8 multiply_add_fusion.1
  323.2 0.9 copy.48
  324.1 0.5 copy-done.1
  324.6 0.9 copy.49
  (32 shorter events, 0.1 us)
Async XLA Ops:
  160.6 152.1 %copy-start.20 = (f32[2,1,96]{2,1,0:T(1,128)S(1)}, f32[2,1,96]{2,1,0:T(1,128)}, u32[]{:S(2)}) copy-start(f32[2,1,96]{2,1,0:T(1,128)} %refs_2_.1) | copy-start | bytes 2308
  160.6 152.1 %copy-start.21 = (f32[2,1,96]{2,1,0:T(1,128)S(1)}, f32[2,1,96]{2,1,0:T(1,128)}, u32[]{:S(2)}) copy-start(f32[2,1,96]{2,1,0:T(1,128)} %param.45) | copy-start | bytes 2308
  160.6 152.1 %copy-start.22 = (f32[2,1,96]{2,1,0:T(1,128)S(1)}, f32[2,1,96]{2,1,0:T(1,128)}, u32[]{:S(2)}) copy-start(f32[2,1,96]{2,1,0:T(1,128)} %param.43) | copy-start | bytes 2308
  160.6 152.1 %copy-start.23 = (f32[2,1,96]{2,1,0:T(1,128)S(1)}, f32[2,1,96]{2,1,0:T(1,128)}, u32[]{:S(2)}) copy-start(f32[2,1,96]{2,1,0:T(1,128)} %param.44) | copy-start | bytes 2308
  160.7 153.5 %copy-start.16 = (f32[2,96,192]{2,1,0:T(8,128)S(1)}, f32[2,96,192]{2,1,0:T(8,128)}, u32[]{:S(2)}) copy-start(f32[2,96,192]{2,1,0:T(8,128)} %refs_6_.1) | copy-start | bytes 442372
  160.7 153.5 %copy-start.17 = (f32[2,96,192]{2,1,0:T(8,128)S(1)}, f32[2,96,192]{2,1,0:T(8,128)}, u32[]{:S(2)}) copy-start(f32[2,96,192]{2,1,0:T(8,128)} %param.33) | copy-start | bytes 442372
  160.7 153.5 %copy-start.18 = (f32[2,96,192]{2,1,0:T(8,128)S(1)}, f32[2,96,192]{2,1,0:T(8,128)}, u32[]{:S(2)}) copy-start(f32[2,96,192]{2,1,0:T(8,128)} %param.31) | copy-start | bytes 442372
  160.7 153.5 %copy-start.19 = (f32[2,96,192]{2,1,0:T(8,128)S(1)}, f32[2,96,192]{2,1,0:T(8,128)}, u32[]{:S(2)}) copy-start(f32[2,96,192]{2,1,0:T(8,128)} %param.32) | copy-start | bytes 442372
  160.7 155.4 %copy-start.13 = (f32[2,96,576]{2,1,0:T(8,128)S(1)}, f32[2,96,576]{2,1,0:T(8,128)}, u32[]{:S(2)}) copy-start(f32[2,96,576]{2,1,0:T(8,128)} %param.28) | copy-start | bytes 1327108
  310.7 5.4 %copy-start.10 = (f32[2,96,576]{2,1,0:T(8,128)S(1)}, f32[2,96,576]{2,1,0:T(8,128)}, u32[]{:S(2)}) copy-start(f32[2,96,576]{2,1,0:T(8,128)} %refs_5_.1) | copy-start | bytes 1327108
  310.7 5.4 %copy-start.11 = (f32[2,96,576]{2,1,0:T(8,128)S(1)}, f32[2,96,576]{2,1,0:T(8,128)}, u32[]{:S(2)}) copy-start(f32[2,96,576]{2,1,0:T(8,128)} %param.29) | copy-start | bytes 1327108
  310.7 5.4 %copy-start.12 = (f32[2,96,576]{2,1,0:T(8,128)S(1)}, f32[2,96,576]{2,1,0:T(8,128)}, u32[]{:S(2)}) copy-start(f32[2,96,576]{2,1,0:T(8,128)} %param.27) | copy-start | bytes 1327108
  316.1 2.8 copy-start.2
  316.1 2.8 copy-start.3
  316.1 2.8 copy-start.4
  316.1 2.8 copy-start.5
  316.2 2.8 copy-start.15
  318.9 1.8 copy-start.6
  318.9 1.8 copy-start.7
  318.9 1.9 copy-start.8
  319.0 2.4 copy-start.9
  319.0 2.5 copy-start.14
  321.5 1.8 copy-start
  323.2 1.4 copy-start.1

commit v2 on v1

--- a/solution.py
+++ b/solution.py
@@ -1214,16 +1214,17 @@
                     w.onward(OUTPUT, layer + 1, i)
 
         feed(x, pl.ds(0, t), lambda i: None)
-        shr_sent.wait()
-        save(n.ws.at[layer], saved[layer].ws)
-        n.hs[layer + 1] = n.mid[layer] + nt(n.act[layer, x], n.ws[layer])
         use = 2 * layer + 1
         part_sent = []
         for number, part in enumerate(parts):
             nb_sent[number].wait()
             feed(y, part, pump if number == 0 else lambda i: None)
+            if number == 0:
+                shr_sent.wait()
             n.psend[use, part, :] = nt(n.act[layer, y, part, :], n.ws[layer]).astype(BF)
             part_sent.append(copies.push(n.psend.at[use, part], n.precv.at[use, part], peer))
+        n.hs[layer + 1] = n.mid[layer] + nt(n.act[layer, x], n.ws[layer])
+        save(n.ws.at[layer], saved[layer].ws)
         for block in range(2):
             n.nb_t[layer, :, block * t : block * t + t] = n.nb[layer, block].T
         save(n.nb_t.at[layer], saved[layer].nb)
@@ -1611,6 +1612,8 @@
     attend_places = (wo, ctx, q, k, v, lse, k_t, wt, na, ctx_t, h)
     top_gl = copies.local(n.gl_h, n.gl.at[LAYERS - 1])
     load(LAYERS - 1, *feed_places, *attend_places)
+    n.squares[...] = jnp.zeros_like(n.squares)
+    mine_at = (w.y, w.z, w.s)
     greet_all(w)
     n.g_out[...] = n.g0[...]
 
@@ -1704,6 +1707,11 @@
         ml_sent = copies.push(n.ml.at[layer, x], n.ml.at[layer, x], peer)
         if layer:
             load(layer - 1, *feed_places)
+        else:
+            n.early[(*mine_at, pl.ds(4, 2))] = rows_b
+            everywhere_start(w, 0, n.early)
+            w.total(EXPAND, 1)
+            w.total(SHRINK, 1)
         n.dk[...] = jnp.zeros_like(n.dk)
         n.dv[...] = jnp.zeros_like(n.dv)
         ready(wo, ctx, q, k, v, lse, k_t)
@@ -1745,13 +1753,18 @@
 
         attend(x, lambda p: None)
         ml_sent.wait()
-        attend(y, lambda p: w.along(EXPAND, layer, p))
+        attend(y, lambda p: None)
         theirs, mine = rows_of(1 - c, t), rows_of(c, t)
         for side in range(2):
             n.kvsend[side, :, pl.ds(0, HALF)] = n.dk[side, theirs, :].astype(BF)
             n.kvsend[side, :, pl.ds(HALF, HALF)] = n.dv[side, theirs, :].astype(BF)
         kv_sent = copies.push(n.kvsend, n.kvrecv.at[layer], sib)
-        w.along(EXPAND, layer, 3)
+        tri_cols, out_cols = pl.ds(0, TRI), pl.ds(TRI, HALF)
+        theirs_too = n.ml[layer, :, :, rows_of(1 - c, HALF)].reshape(2 * t, HALF)
+        ready(ctx_t)
+        n.gs_shr[:, out_cols] = nn(n.ctx_t[...], theirs_too).astype(BF)
+        out_sent = copies.push(n.gs_shr.at[:, out_cols], n.gr_att.at[:, out_cols], sib)
+        w.along_all(EXPAND, layer)
 
         def unturn(block, j, value):
             cosine, sine = n.cs[block, :, 0:128], n.cs[block, :, 128:256]
@@ -1769,61 +1782,56 @@
                 n.pg[side, :, pl.ds(D + 128 * j, 128)] = (
                     n.dv[side, mine, at] + n.kvrecv[layer, side, :, pl.ds(HALF + 128 * j, 128)].astype(F32)
                 ).astype(BF)
-        ready(wt, na, ctx_t, h)
+        ready(wt, na, h)
         use = 2 * layer + 1
         n.psend[...] = nt(n.pg[y], n.wt[...]).astype(BF)
         part_sent = copies.push(n.psend, n.precv.at[use], peer)
         rows = D // dp
-
-        def send_tri(i, carry):
-            pl.when(i < 2)(lambda: w.along(SHRINK, layer, i))
-            off = pl.ds(pl.multiple_of((1 - c) * HALF + i * rows, rows), rows)
-            n.gs_shr[rows_of(i, rows), pl.ds(0, TRI)] = nn(n.na[off, :], n.pg[...].reshape(2 * t, TRI)).astype(BF)
-            return carry
-
-        lax.fori_loop(0, w.zs, send_tri, 0)
-        tri_cols, out_cols = pl.ds(0, TRI), pl.ds(TRI, HALF)
-        tri_sent = copies.push(n.gs_shr.at[:, tri_cols], n.gr_att.at[:, tri_cols], sib)
-        theirs_too = n.ml[layer, :, :, rows_of(1 - c, HALF)].reshape(2 * t, HALF)
-        n.gs_shr[:, out_cols] = nn(n.ctx_t[...], theirs_too).astype(BF)
-        out_sent = copies.push(n.gs_shr.at[:, out_cols], n.gr_att.at[:, out_cols], sib)
-        n.part[...] = nt(n.pg[x], n.wt[...])
-        tri_sent.wait()
-
-        def keep_tri(i, carry):
-            at = rows_of(i, rows)
-            row_block = n.na[pl.ds(pl.multiple_of(c * HALF + i * rows, rows), rows), :]
-            value = nn(row_block, n.pg[...].reshape(2 * t, TRI)) + n.gr_att[at, tri_cols].astype(F32)
-            n.gt[layer, at, :] = value.astype(BF)
-            return carry
-
-        lax.fori_loop(0, w.zs, keep_tri, 0)
-        w.across_all(TRIPLE, layer)
         out_sent.wait()
         mine_too = n.ml[layer, :, :, rows_of(c, HALF)].reshape(2 * t, HALF)
         value = nn(n.ctx_t[...], mine_too) + n.gr_att[:, out_cols].astype(F32)
         n.go[layer] = value.astype(BF)
         w.across_all(OUTPUT, layer)
+
+        def send_tri(i, carry):
+            off = pl.ds(pl.multiple_of((1 - c) * HALF + i * rows, rows), rows)
+            n.gs_shr[rows_of(i, rows), pl.ds(0, TRI)] = nn(n.na[off, :], n.pg[...].reshape(2 * t, TRI)).astype(BF)
+            return carry
+
+        lax.fori_loop(0, w.zs, send_tri, 0)
+        tri_sent = copies.push(n.gs_shr.at[:, tri_cols], n.gr_att.at[:, tri_cols], sib)
+        n.part[...] = nt(n.pg[x], n.wt[...])
+        tri_sent.wait()
+
+        def keep_tri(i, carry):
+            block = 2 * lax.rem(i, 2) + jnp.where(i < 2, 1 - w.y, w.y)
+            at = rows_of(block, rows)
+            row_block = n.na[pl.ds(pl.multiple_of(c * HALF + block * rows, rows), rows), :]
+            value = nn(row_block, n.pg[...].reshape(2 * t, TRI)) + n.gr_att[at, tri_cols].astype(F32)
+            n.gt[layer, at, :] = value.astype(BF)
+            return carry
+
+        lax.fori_loop(0, 2, keep_tri, 0)
+        w.across_all(TRIPLE, layer)
+        w.along_all(SHRINK, layer)
+        lax.fori_loop(2, w.zs, keep_tri, 0)
         part_sent.wait()
         dy = n.part[...] + n.precv[use].astype(F32)
         back_h, rows_a = norm_back(n.h[...], n.sc[layer, 0:1, :], dy)
         n.g_out[...] = n.g_out[...] + back_h
-        mine_at = (w.y, w.z, w.s)
         if layer:
             load(layer - 1, *attend_places)
             n.early[(*mine_at, pl.ds(0, 2))] = rows_a
             n.early[(*mine_at, pl.ds(2, 2))] = rows_b
         else:
-            n.early[(*mine_at, pl.ds(4, 2))] = rows_b
             n.late[mine_at] = rows_a
 
-    everywhere_start(w, 0, n.early)
+    w.along_all(OUTPUT, 0)
+    w.along(TRIPLE, 0, 0)
     everywhere_start(w, 1, n.late)
-    n.squares[...] = jnp.zeros_like(n.squares)
-    for kind in (EXPAND, SHRINK, TRIPLE, OUTPUT):
+    w.along(TRIPLE, 0, 1)
+    for kind in (TRIPLE, OUTPUT):
         w.total(kind, 1)
-    w.along_all(TRIPLE, 0)
-    w.along_all(OUTPUT, 0)
     for kind in (EXPAND, SHRINK):
         w.total(kind, 0)
     first = everywhere_end(w, 0, n.early, n.early_pair)

time: 330 us -> 329 us (level)
  no operation moved by 1% of the time
where the time goes in v2:
time: 329 us; the launch traced here: 327 us
  Pallas kernels  305 us (93%)
  other arithmetic  11.4 us (3%)
  local copies, waits for them, and re-layouts  5.77 us (2%)
  between operations  4.37 us (1%)
    pallas_call x1, Pallas kernels, forward_all(): pl.pallas_call(functools.partial(fwd_kernel, dp), name='forward', out_sha...  154 us
    pallas_call x1, Pallas kernels, backward_all(): pl.pallas_call(functools.partial(bwd_kernel, dp), name='backward', out_sh...  151 us
    add x5, other arithmetic, adam_step(): average = shadow_decay * shadow + (1.0 - shadow_decay) * updated  9.55 us

profile of v2, /device:TPU:0, one launch (start us, length us, event | category | flops | bytes accessed | tf_op | source)
XLA Modules:
  0.0 326.7 jit_solution(4692749511160463576)
XLA Ops:
  0.7 1.3 fusion.17
  3.4 1.0 multiply_cosine_fusion
  4.4 0.8 pad_maximum_fusion.refs_3_
  5.2 154.3 %forward.1 = (f32[256,768]{1,0:T(8,128)}, f32[256,768]{1,0:T(8,128)}, f32[256,768]{1,0:T(8,128)}, f32[256,768]{1,0:T(8,128)}, f32[2,4,768]{2,1,0:T(4,128)}, /*in...) custom-call(f32[256,768]{1,0:T(8,128)} %refs_20_.1, ...), custom_call_target="tpu_custom_call" | custom-call | flops 23622320128 | bytes 33554432 | tf_op jit(solution)/shard_map/forward/pallas_call | solution.py:1289
  159.5 0.0 copy-start.20
  159.5 0.0 copy-start.21
  159.5 0.0 copy-start.22
  159.5 0.0 copy-start.23
  159.5 0.0 copy-start.16
  159.5 0.0 copy-start.17
  159.5 0.0 copy-start.18
  159.5 0.0 copy-start.19
  159.6 0.0 copy-start.13
  159.6 150.9 %backward.1 = (f32[256,768]{1,0:T(8,128)}, f32[2,4,768]{2,1,0:T(4,128)}, f32[8,128]{1,0:T(8,128)}, f32[2,96,576]{2,1,0:T(8,128)}, f32[2,96,192]{2,1,0:T(8,128)},...) custom-call(f32[256,768]{1,0:T(8,128)} %refs_0_.3, bf16[2,256,768]{2,1,0:T(8,128)(2,1)} %get-tuple-element.67.refs_1_, ...), custom_call_target="tpu_custom_call" | custom-call | flops 47244640256 | bytes 50331648 | tf_op jit(solution)/shard_map/backward/pallas_call | solution.py:1918
  310.5 0.0 copy-start.10
  310.5 0.0 copy-start.11
  310.5 1.3 slice.11
  312.6 1.4 multiply_add_fusion.7
  314.0 1.9 multiply_add_fusion.5
  316.0 0.0 copy-start.3
  316.0 0.0 copy-start.4
  316.0 2.7 multiply_add_fusion.3
  318.8 0.0 copy-start.8
  318.8 0.0 copy-start.9
  318.8 1.8 multiply_add_fusion
  320.6 0.1 copy-done.8
  320.7 0.6 copy-done.9
  321.2 0.1 copy-done.14
  321.3 1.8 multiply_add_fusion.1
  323.1 0.9 copy.48
  324.0 0.5 copy-done.1
  324.5 0.9 copy.49
  (32 shorter events, 0.1 us)
Async XLA Ops:
  159.5 153.1 %copy-start.20 = (f32[2,1,96]{2,1,0:T(1,128)S(1)}, f32[2,1,96]{2,1,0:T(1,128)}, u32[]{:S(2)}) copy-start(f32[2,1,96]{2,1,0:T(1,128)} %refs_2_.1) | copy-start | bytes 2308
  159.5 153.1 %copy-start.21 = (f32[2,1,96]{2,1,0:T(1,128)S(1)}, f32[2,1,96]{2,1,0:T(1,128)}, u32[]{:S(2)}) copy-start(f32[2,1,96]{2,1,0:T(1,128)} %param.45) | copy-start | bytes 2308
  159.5 153.1 %copy-start.22 = (f32[2,1,96]{2,1,0:T(1,128)S(1)}, f32[2,1,96]{2,1,0:T(1,128)}, u32[]{:S(2)}) copy-start(f32[2,1,96]{2,1,0:T(1,128)} %param.43) | copy-start | bytes 2308
  159.5 153.1 %copy-start.23 = (f32[2,1,96]{2,1,0:T(1,128)S(1)}, f32[2,1,96]{2,1,0:T(1,128)}, u32[]{:S(2)}) copy-start(f32[2,1,96]{2,1,0:T(1,128)} %param.44) | copy-start | bytes 2308
  159.5 154.5 %copy-start.16 = (f32[2,96,192]{2,1,0:T(8,128)S(1)}, f32[2,96,192]{2,1,0:T(8,128)}, u32[]{:S(2)}) copy-start(f32[2,96,192]{2,1,0:T(8,128)} %refs_6_.1) | copy-start | bytes 442372
  159.5 154.5 %copy-start.17 = (f32[2,96,192]{2,1,0:T(8,128)S(1)}, f32[2,96,192]{2,1,0:T(8,128)}, u32[]{:S(2)}) copy-start(f32[2,96,192]{2,1,0:T(8,128)} %param.33) | copy-start | bytes 442372
  159.5 154.5 %copy-start.18 = (f32[2,96,192]{2,1,0:T(8,128)S(1)}, f32[2,96,192]{2,1,0:T(8,128)}, u32[]{:S(2)}) copy-start(f32[2,96,192]{2,1,0:T(8,128)} %param.31) | copy-start | bytes 442372
  159.5 154.5 %copy-start.19 = (f32[2,96,192]{2,1,0:T(8,128)S(1)}, f32[2,96,192]{2,1,0:T(8,128)}, u32[]{:S(2)}) copy-start(f32[2,96,192]{2,1,0:T(8,128)} %param.32) | copy-start | bytes 442372
  159.6 156.4 %copy-start.13 = (f32[2,96,576]{2,1,0:T(8,128)S(1)}, f32[2,96,576]{2,1,0:T(8,128)}, u32[]{:S(2)}) copy-start(f32[2,96,576]{2,1,0:T(8,128)} %param.28) | copy-start | bytes 1327108
  310.5 5.4 %copy-start.10 = (f32[2,96,576]{2,1,0:T(8,128)S(1)}, f32[2,96,576]{2,1,0:T(8,128)}, u32[]{:S(2)}) copy-start(f32[2,96,576]{2,1,0:T(8,128)} %refs_5_.1) | copy-start | bytes 1327108
  310.5 5.4 %copy-start.11 = (f32[2,96,576]{2,1,0:T(8,128)S(1)}, f32[2,96,576]{2,1,0:T(8,128)}, u32[]{:S(2)}) copy-start(f32[2,96,576]{2,1,0:T(8,128)} %param.29) | copy-start | bytes 1327108
  310.5 5.4 %copy-start.12 = (f32[2,96,576]{2,1,0:T(8,128)S(1)}, f32[2,96,576]{2,1,0:T(8,128)}, u32[]{:S(2)}) copy-start(f32[2,96,576]{2,1,0:T(8,128)} %param.27) | copy-start | bytes 1327108
  315.9 2.8 copy-start.2
  316.0 2.8 copy-start.3
  316.0 2.8 copy-start.4
  316.0 2.8 copy-start.5
  316.0 2.8 copy-start.15
  318.8 1.8 copy-start.6
  318.8 1.8 copy-start.7
  318.8 1.9 copy-start.8
  318.8 2.4 copy-start.9
  318.8 2.5 copy-start.14
  321.3 1.8 copy-start
  323.1 1.4 copy-start.1
